TPU v7x, 128 devices: a whole 4x4x4 slice. The times are simulated.
128 devices in a mesh: comm: 4 (over x), wide: 32 (over y, z, core).
Axes of the slice: x: 4, y: 4, z: 4, core: 2. Of those that a mesh axis runs over, the one named last changes fastest.
Arguments:
- feats: bfloat16 [256, 768, 768], P(('comm', 'wide')), may hold values from -6 to 6
- tiles: bfloat16 [256, 3, 768, 768], P(('comm', 'wide')), may hold values from -0.15625 to 0.15625
- tile_src: int32 [256, 3], P(('comm', 'wide')), may hold values from 0 to 5
- tile_count: int32 [256], P(('comm', 'wide')), may hold values from 1 to 3
- request: int32 [128, 4], P(('comm', 'wide')), may hold values from 0 to 1
- z_old: bfloat16 [256, 768, 1024], P(('comm', 'wide')), may hold values from -6 to 6
- dual: bfloat16 [256, 768, 1024], P(('comm', 'wide')), may hold values from -6 to 6
- target: bfloat16 [256, 768, 1024], P(('comm', 'wide')), may hold values from 0 to 2
- w_rows: bfloat16 [768, 1024], P('wide'), may hold values from -0.21875 to 0.21875
- rho: float32 [1024], replicated, may hold values from 0.3 to 4
- beta: float32 [1024], replicated, may hold values from 0.3 to 4
Outputs:
- new_z: bfloat16 [256, 768, 1024], P(('comm', 'wide'))
- new_dual: bfloat16 [256, 768, 1024], P(('comm', 'wide'))
- weight_grad: float32 [768, 1024], P('wide')
Inputs may be any that keep to these rules, and one draw needn't show every extreme that they name: `tile_src`: entries beyond tile_count of a community are not read.
All inputs are finite; a program needn't handle non-finite values.
Results may differ from a plain program's by a relative error of at most 0.0095.
Values may be sent and summed in bfloat16 or wider, within the bound.
No kernel may reach another device: no remote copies, remote signals or barrier semaphores. Data moves between devices by JAX's collectives and lax.ppermute only.
A program may use at most 128 MiB of HBM per device.

v0:
```python
import math

import jax
import jax.numpy as jnp
from jax import lax
from jax.sharding import PartitionSpec as P


def cut_along(shard, dim, size):
    before, after = (shard.shape[:dim], shard.shape[dim + 1 :])
    return jnp.moveaxis(shard.reshape(*before, size, -1, *after), dim, 0)


def summed_on_arrival(shard, axis, dim):
    tiles = cut_along(shard, dim, lax.axis_size(axis))
    arrived = lax.all_to_all(tiles, axis, split_axis=0, concat_axis=0, tiled=True)
    return arrived.astype(jnp.float32).sum(axis=0)


def total_of_pieces(shard, axis):
    tiles = lax.all_gather(shard, axis).astype(jnp.float32)
    return tiles.sum(axis=0)


def tile_product(tile, source, alive, feats, peer_pool, peer_index):
    own_count = feats.shape[0]

    def from_own():
        block = lax.dynamic_index_in_dim(
            feats, jnp.minimum(source, own_count - 1), 0, keepdims=False
        )
        return jnp.dot(tile, block, preferred_element_type=jnp.float32)

    def from_peer():
        which = peer_index(jnp.maximum(source - own_count, 0))
        block = lax.dynamic_index_in_dim(peer_pool, which, 0, keepdims=False)
        return jnp.dot(tile, block, preferred_element_type=jnp.float32)

    def skipped():
        return jnp.zeros((tile.shape[0], feats.shape[2]), jnp.float32)

    def live_product():
        return lax.cond(source < own_count, from_own, from_peer)

    return lax.cond(alive, live_product, skipped)


def local(feats, tiles, tile_src, tile_count, request, z_old, dual, target, w_rows, rho, beta):
    local_comms, nodes, width = feats.shape
    hidden = w_rows.shape[1]
    tile_slots = tiles.shape[1]
    group_size = lax.axis_size("comm")
    wanted = lax.all_to_all(request, "comm", split_axis=1, concat_axis=0, tiled=True)
    outgoing = feats[wanted[:, 0]]
    peer_pool = lax.all_to_all(outgoing, "comm", split_axis=0, concat_axis=0, tiled=True)

    def peer_index(member):
        return member

    results = []
    for comm_pos in range(local_comms):
        total = jnp.zeros((nodes, width), jnp.float32)
        for tile_pos in range(tile_slots):
            alive = tile_pos < tile_count[comm_pos]
            total = total + tile_product(
                tiles[comm_pos, tile_pos],
                tile_src[comm_pos, tile_pos],
                alive,
                feats,
                peer_pool,
                peer_index,
            )
        results.append(total.astype(jnp.bfloat16))
    flat = jnp.concatenate(results, 0)
    columns = flat
    pre = jnp.dot(
        columns,
        lax.all_gather(w_rows, "wide", axis=0, tiled=True),
        preferred_element_type=jnp.float32,
    )
    pre = pre.reshape(local_comms, nodes, hidden)
    shifted = pre + dual.astype(jnp.float32) / rho
    active = (rho * shifted + beta * target.astype(jnp.float32)) / (rho + beta)
    znew = jnp.where(z_old > 0, active, shifted)
    new_dual = (dual.astype(jnp.float32) + rho * (pre - znew)).astype(jnp.bfloat16)
    dual_flat = new_dual.reshape(-1, hidden)
    total_nodes = local_comms * nodes * group_size * lax.axis_size("wide")
    factor = 1.0 / math.sqrt(total_nodes)
    columns = flat
    partial_rows = summed_on_arrival(
        jnp.einsum("nf,nh->fh", columns, dual_flat, preferred_element_type=jnp.float32).astype(
            jnp.bfloat16
        ),
        "wide",
        0,
    )
    grad = total_of_pieces(partial_rows.astype(jnp.bfloat16), "comm").astype(jnp.float32)
    return (znew.astype(jnp.bfloat16), new_dual, grad * factor)


def solution(mesh):
    in_specs = (
        P(("comm", "wide"), None, None),
        P(("comm", "wide"), None, None, None),
        P(("comm", "wide"), None),
        P(("comm", "wide")),
        P(("comm", "wide"), None),
        P(("comm", "wide"), None, None),
        P(("comm", "wide"), None, None),
        P(("comm", "wide"), None, None),
        P("wide", None),
        P(),
        P(),
    )
    out_specs = (P(("comm", "wide"), None, None), P(("comm", "wide"), None, None), P("wide", None))
    return jax.shard_map(local, mesh=mesh, in_specs=in_specs, out_specs=out_specs, check_vma=False)
```

profile of v0, /device:TPU:0, one launch (start us, length us, event | category | flops | bytes accessed | tf_op | source)
XLA Modules:
  0.0 185.7 jit_solution(2910272487670939160)
XLA Ops:
  7.9 9.4 %all_to_all.23 = s32[1,4,1]{2,0,1:T(1,128)S(1)} all-to-all(s32[1,4,1]{2,0,1:T(1,128)S(1)} %copy.16), channel_id=1, replica_groups=mesh['comm'=4,'wide'=32] {'comm'}, dimensions={1} | all-to-all | bytes 32 | tf_op jit(solution)/shard_map/all_to_all | solution.py:53
  17.5 4.7 %gather_fusion = bf16[4,768,768]{2,1,0:T(8,128)(2,1)} fusion(bf16[2,768,768]{2,1,0:T(8,128)(2,1)} %param.35, s32[1024]{0:T(1024)S(1)} %pad_clamp_fusion), kind=kCustom, calls=%fused_computation | custom fusion | bytes 9437200 | tf_op jit(solution)/shard_map/gather | solution.py:54
  22.2 5.1 %all-to-all-start.1 = ((bf16[4,768,768]{2,1,0:T(8,128)(2,1)}), bf16[4,768,768]{2,1,0:T(8,128)(2,1)}, u32[]{:S(2)}, u32[]{:S(2)}) async-start(bf16[4,768,768]{2,1,0:T(8,128)(2,1)} %gather_fusion), calls=%async_computation.1 | async-start | bytes 9437184 | tf_op jit(solution)/shard_map/all_to_all | solution.py:55
  32.6 48.1 %all-to-all-done.1 = bf16[4,768,768]{2,1,0:T(8,128)(2,1)} async-done(((bf16[4,768,768]{2,1,0:T(8,128)(2,1)}), bf16[4,768,768]{2,1,0:T(8,128)(2,1)}, u32[]{:S(2)}, u32[]{:S(2)}) %all-to-all-start.1) | async-done | bytes 4718624 | tf_op jit(solution)/shard_map/all_to_all | solution.py:55
  80.6 7.0 %conditional.12 = (f32[768,768]{0,1:T(8,128)}) conditional(s32[]{:T(128)} %bitcast.36, () %tuple.80, (s32[2,3]{1,0:T(2,128)S(1)}, bf16[2,3,768,768]{3,2,1,0:T(8,128)(2,1)}, bf16[4,768,768]{2,1,0:T(8,128)(2,1)}, bf16[2,768,768]{2,1,0:T(8,128)(2,1)S(1)}) %tuple.123), branch_computations={%region_0.0_spmd, %region_1.4_spmd} | conditional | flops 905969664 | bytes 7078016 | solution.py:45
  83.2 4.5 %conditional = (f32[768,768]{0,1:T(8,128)}) conditional(s32[]{:T(128)} %convert_element_type.55, (s32[]{:T(128)}, bf16[4,768,768]{2,1,0:T(8,128)(2,1)}, bf16[768,768]{1,0:T(8,128)(2,1)S(1)}) %tuple.54, (s32[]{:T(128)}, bf16[2,768,768]{2,1,0:T(8,128)(2,1)S(1)}, bf16[768,768]{1,0:T(8,128)(2,1)S(1)}) %tuple.55), branch_computations={%region_2.2_spmd, %region_3.3_spmd} | conditional | flops 905969664 | bytes 4718650 | solution.py:43
  83.8 3.8 %convolution_bitcast_fusion = f32[768,768]{0,1:T(8,128)} fusion(bf16[768,768]{1,0:T(8,128)(2,1)S(1)} %get-tuple-element.182, bf16[4,768,768]{2,1,0:T(8,128)(2,1)} %get-tuple-element.180, s32[]{:T(128)S(6)} %max.12), kind=kOutput, calls=%fused_computation.1 | convolution fusion | flops 905969664 | bytes 4718596 | tf_op jit(solution)/shard_map/cond/branch_1_fun/cond/branch_0_fun/dot_general | solution.py:37
  87.7 1.6 conditional.13
  87.7 1.6 broadcast.34
  89.3 1.5 conditional.14
  90.8 7.1 %conditional.15 = (f32[768,768]{0,1:T(8,128)}) conditional(s32[]{:T(128)} %bitcast.41, () %tuple.84, (s32[2,3]{1,0:T(2,128)S(1)}, bf16[2,3,768,768]{3,2,1,0:T(8,128)(2,1)}, bf16[4,768,768]{2,1,0:T(8,128)(2,1)}, bf16[2,768,768]{2,1,0:T(8,128)(2,1)S(1)}) %tuple.126), branch_computations={%region_12.13_spmd, %region_13.16_spmd} | conditional | flops 905969664 | bytes 7078016 | solution.py:45
  93.4 4.5 %conditional.3 = (f32[768,768]{0,1:T(8,128)}) conditional(s32[]{:T(128)} %convert_element_type.58, (s32[]{:T(128)}, bf16[4,768,768]{2,1,0:T(8,128)(2,1)}, bf16[768,768]{1,0:T(8,128)(2,1)S(1)}) %tuple.60, (s32[]{:T(128)}, bf16[2,768,768]{2,1,0:T(8,128)(2,1)S(1)}, bf16[768,768]{1,0:T(8,128)(2,1)S(1)}) %tuple.61), branch_computations={%region_14.14_spmd, %region_15.15_spmd} | conditional | flops 905969664 | bytes 4718650 | solution.py:43
  94.1 3.8 %convolution_bitcast_fusion.6 = f32[768,768]{0,1:T(8,128)} fusion(bf16[768,768]{1,0:T(8,128)(2,1)S(1)} %get-tuple-element.212, bf16[4,768,768]{2,1,0:T(8,128)(2,1)} %get-tuple-element.210, s32[]{:T(128)S(6)} %max.15), kind=kOutput, calls=%fused_computation.28 | convolution fusion | flops 905969664 | bytes 4718596 | tf_op jit(solution)/shard_map/cond/branch_1_fun/cond/branch_0_fun/dot_general | solution.py:37
  97.9 7.1 %conditional.16 = (f32[768,768]{0,1:T(8,128)}) conditional(s32[]{:T(128)} %bitcast.42, () %tuple.85, (s32[2,3]{1,0:T(2,128)S(1)}, bf16[2,3,768,768]{3,2,1,0:T(8,128)(2,1)}, bf16[4,768,768]{2,1,0:T(8,128)(2,1)}, bf16[2,768,768]{2,1,0:T(8,128)(2,1)S(1)}) %tuple.127), branch_computations={%region_16.17_spmd, %region_17.20_spmd} | conditional | flops 905969664 | bytes 7078016 | solution.py:45
  100.5 4.5 %conditional.4 = (f32[768,768]{0,1:T(8,128)}) conditional(s32[]{:T(128)} %convert_element_type.59, (s32[]{:T(128)}, bf16[4,768,768]{2,1,0:T(8,128)(2,1)}, bf16[768,768]{1,0:T(8,128)(2,1)S(1)}) %tuple.62, (s32[]{:T(128)}, bf16[2,768,768]{2,1,0:T(8,128)(2,1)S(1)}, bf16[768,768]{1,0:T(8,128)(2,1)S(1)}) %tuple.63), branch_computations={%region_18.18_spmd, %region_19.19_spmd} | conditional | flops 905969664 | bytes 4718650 | solution.py:43
  101.2 3.9 %convolution_bitcast_fusion.8 = f32[768,768]{0,1:T(8,128)} fusion(bf16[768,768]{1,0:T(8,128)(2,1)S(1)} %get-tuple-element.222, bf16[4,768,768]{2,1,0:T(8,128)(2,1)} %get-tuple-element.220, s32[]{:T(128)S(6)} %max.16), kind=kOutput, calls=%fused_computation.37 | convolution fusion | flops 905969664 | bytes 4718596 | tf_op jit(solution)/shard_map/cond/branch_1_fun/cond/branch_0_fun/dot_general | solution.py:37
  105.0 1.6 conditional.17
  105.0 1.6 broadcast.38
  106.6 5.8 %add_convert_fusion = (bf16[768,768]{0,1:T(8,128)(2,1)S(1)}, bf16[768,768]{0,1:T(8,128)(2,1)S(1)}) fusion(f32[768,768]{0,1:T(8,128)} %get-tuple-element.260, f32[768,768]{0,1:T(8,128)} %get-tuple-element.258, f32[768,768]{0,1:T(8,128)} %get-tuple-element.259, f32[768,768]{0,1:T(8,128)} %get-tuple-element.257, f32[768,768]{0,1:T(8,128)} %get-tuple-element.255, ...), kind=kLoop, calls=%fused_computation.61 | loop fusion | flops 3538944 | bytes 16515072 | tf_op jit(solution)/shard_map/convert_element_type | solution.py:73
  112.5 4.2 %fusion.38 = f32[1536,1024]{1,0:T(8,128)S(1)} fusion(bf16[768,1024]{1,0:T(8,128)(2,1)} %all-gather.3.cloned.1.call-done, bf16[768,768]{0,1:T(8,128)(2,1)S(1)} %get-tuple-element.247, bf16[768,768]{0,1:T(8,128)(2,1)S(1)} %get-tuple-element.248), kind=kOutput, calls=%fused_computation.64 | convolution fusion | flops 2420637696 | bytes 10223616 | tf_op jit(solution)/shard_map/dot_general | solution.py:76
  116.8 4.6 %fusion.37 = (bf16[2,768,1024]{2,1,0:T(8,128)(2,1)S(1)}, bf16[2,768,1024]{2,1,0:T(8,128)(2,1)}) fusion(bf16[2,768,1024]{2,1,0:T(8,128)(2,1)S(1)} %copy-done.1, f32[2,768,1024]{2,1,0:T(8,128)S(1)} %bitcast.108, f32[1024]{0:T(1024)S(1)} %copy-done.5, f32[1024]{0:T(1024)S(1)} %add.73, bf16[2,768,1024]{2,1,0:T(8,128)(2,1)S(1)} %copy-done.2, ...), kind=kLoop, calls=%fused_computation.58 | loop fusion | flops 23592960 | bytes 22032384 | tf_op jit(solution)/shard_map/convert_element_type | solution.py:85
  121.4 2.6 %convolution_convert_fusion = bf16[768,1024]{1,0:T(8,128)(2,1)S(1)} fusion(bf16[1536,1024]{1,0:T(8,128)(2,1)S(1)} %bitcast.109, bf16[768,768]{0,1:T(8,128)(2,1)S(1)} %get-tuple-element.247, bf16[768,768]{0,1:T(8,128)(2,1)S(1)} %get-tuple-element.248), kind=kOutput, calls=%fused_computation.63 | convolution fusion | flops 2421424128 | bytes 7077888 | tf_op jit(solution)/shard_map/nf,nh->fh/dot_general | solution.py:91
  124.0 41.7 %all_to_all.24 = bf16[32,24,1024]{2,1,0:T(8,128)(2,1)S(1)} all-to-all(bf16[32,24,1024]{2,1,0:T(8,128)(2,1)S(1)} %bitcast.110), channel_id=1, replica_groups=mesh['comm'=4,'wide'=32] {'wide'}, dimensions={0} | all-to-all | bytes 3145728 | tf_op jit(solution)/shard_map/all_to_all | solution.py:16
  166.0 12.2 %all-gather = bf16[96,1024]{1,0:T(8,128)(2,1)S(1)} all-gather(bf16[24,1024]{1,0:T(8,128)(2,1)S(1)} %reduce_sum.21), channel_id=2, replica_groups=mesh['comm'=4,'wide'=32] {'comm'}, dimensions={0}, use_global_device_ids=true | all-gather | bytes 245760 | tf_op jit(solution)/shard_map/all_gather | solution.py:21
  (37 shorter events, 10.6 us)
Async XLA Ops:
  22.2 5.9 %copy-start.7 = (s32[2]{0:T(128)S(1)}, s32[2]{0:T(128)}, u32[]{:S(2)}) copy-start(s32[2]{0:T(128)} %param.38) | copy-start | bytes 28
  22.2 10.3 %copy-start.5 = (f32[1024]{0:T(1024)S(1)}, f32[1024]{0:T(1024)}, u32[]{:S(2)}) copy-start(f32[1024]{0:T(1024)} %param.44) | copy-start | bytes 12292
  22.2 10.3 %copy-start.6 = (f32[1024]{0:T(1024)S(1)}, f32[1024]{0:T(1024)}, u32[]{:S(2)}) copy-start(f32[1024]{0:T(1024)} %param.45) | copy-start | bytes 12292
  22.2 58.4 %copy-start = (bf16[2,768,768]{2,1,0:T(8,128)(2,1)S(1)}, bf16[2,768,768]{2,1,0:T(8,128)(2,1)}, u32[]{:S(2)}) copy-start(bf16[2,768,768]{2,1,0:T(8,128)(2,1)} %param.35) | copy-start | bytes 7077892
  22.2 58.4 %copy-start.8 = (s32[2,3]{1,0:T(2,128)S(1)}, s32[2,3]{1,0:T(2,128)}, u32[]{:S(2)}) copy-start(s32[2,3]{1,0:T(2,128)} %param.37) | copy-start | bytes 76
  22.2 58.4 %all-to-all-start.1 = ((bf16[4,768,768]{2,1,0:T(8,128)(2,1)}), bf16[4,768,768]{2,1,0:T(8,128)(2,1)}, u32[]{:S(2)}, u32[]{:S(2)}) async-start(bf16[4,768,768]{2,1,0:T(8,128)(2,1)} %gather_fusion), calls=%async_computation.1 | async-start | bytes 9437184 | tf_op jit(solution)/shard_map/all_to_all | solution.py:55
  27.3 85.1 %all-gather.3.cloned.1.call-start = ((), (), s32[]{:S(2)}) async-start(), calls=%async_computation.3 | async-start | bytes 1622016 | tf_op jit(solution)/shard_map/all_gather | solution.py:78
  112.4 4.3 %copy-start.1 = (bf16[2,768,1024]{2,1,0:T(8,128)(2,1)S(1)}, bf16[2,768,1024]{2,1,0:T(8,128)(2,1)}, u32[]{:S(2)}) copy-start(bf16[2,768,1024]{2,1,0:T(8,128)(2,1)} %param.41) | copy-start | bytes 9437188
  112.5 4.3 %copy-start.2 = (bf16[2,768,1024]{2,1,0:T(8,128)(2,1)S(1)}, bf16[2,768,1024]{2,1,0:T(8,128)(2,1)}, u32[]{:S(2)}) copy-start(bf16[2,768,1024]{2,1,0:T(8,128)(2,1)} %param.42) | copy-start | bytes 9437188
  112.5 4.3 %copy-start.3 = (bf16[2,768,1024]{2,1,0:T(8,128)(2,1)S(1)}, bf16[2,768,1024]{2,1,0:T(8,128)(2,1)}, u32[]{:S(2)}) copy-start(bf16[2,768,1024]{2,1,0:T(8,128)(2,1)} %param.40) | copy-start | bytes 9437188
  121.4 2.6 %copy-start.4 = (bf16[2,768,1024]{2,1,0:T(8,128)(2,1)}, bf16[2,768,1024]{2,1,0:T(8,128)(2,1)S(1)}, u32[]{:S(2)}) copy-start(bf16[2,768,1024]{2,1,0:T(8,128)(2,1)S(1)} %get-tuple-element.243) | copy-start | bytes 9437188
Sparse Core Ops, SparseCore 0:
  30.4 46.1 all-gather.2
where the time goes:
time: 189 us; the launch traced here: 186 us
  blocking collectives  63.3 us (33%)
  waiting for transfers between devices  48.8 us (26%)
  matrix products  18.4 us (10%)
  between operations  18.1 us (10%)
  local copies, waits for them, and re-layouts  16.5 us (9%)
  other arithmetic  11.6 us (6%)
  starting transfers between devices  5.12 us (3%)
  loops' own time  3.95 us (2%)
    all_to_all x1, waiting for transfers between devices, local(): lax.all_to_all(outgoing, 'comm', split_axis=0, concat_axis=0, tiled=True)  48.1 us
    all_to_all x1, blocking collectives, summed_on_arrival(): lax.all_to_all(tiles, axis, split_axis=0, concat_axis=0, tiled=True)  41.7 us
    all_gather x1, blocking collectives, total_of_pieces(): tiles = lax.all_gather(shard, axis).astype(jnp.float32)  12.2 us
    dot_general x3, matrix products, from_peer(): return jnp.dot(tile, block, preferred_element_type=jnp.float32)  11.5 us
    all_to_all x1, blocking collectives, local(): lax.all_to_all(request, 'comm', split_axis=1, concat_axis=0, tiled=True)  9.42 us
    convert_element_type x1, other arithmetic, local(): results.append(total.astype(jnp.bfloat16))  5.83 us
    all_to_all x1, starting transfers between devices, local(): lax.all_to_all(outgoing, 'comm', split_axis=0, concat_axis=0, tiled=True)  5.08 us
    another operation x3, local copies, waits for them, and re-layouts  4.72 us
  transfers between devices with their start and end apart: 2, of which 1 were waited for; matrix products, arithmetic and copies ran while one was open for 15% of the time, Pallas kernels for 0%

commit v1 on v0

v1 whole, which is shorter than its diff:
```python
import functools
import math

import jax
import jax.numpy as jnp
from jax import lax
from jax.experimental import pallas as pl
from jax.experimental.pallas import tpu as pltpu
from jax.sharding import PartitionSpec as P

ROWS = 256
COLS = 256
LIMIT = 24 * 2**20
SMEM = pl.BlockSpec(memory_space=pltpu.SMEM)
VMEM = pl.BlockSpec(memory_space=pltpu.VMEM)
ANY = pl.BlockSpec(memory_space=pl.ANY)


def shifted(x, axis, to):
    size = lax.axis_size(axis)
    return lax.ppermute(x, axis, [(i, to(i)) for i in range(size)])


def place(w):
    return w // 8, w // 2 % 4, w % 2


def along_comm(x, step):
    return shifted(x, "comm", lambda i: (i + step) % 4)


def along_core(x):
    return shifted(x, "wide", lambda w: w ^ 1)


def along_z(x, step):
    return shifted(x, "wide", lambda w: w // 8 * 8 + (w // 2 % 4 + step) % 4 * 2 + w % 2)


def along_y(x, step):
    return shifted(x, "wide", lambda w: (w // 8 + step) % 4 * 8 + w % 8)


def own_products(src, count, request, feats, tiles, acc, buf, sems):
    me = lax.axis_index("comm")
    comms, slots = tiles.shape[0], tiles.shape[1]
    local = feats.shape[0]

    def wanted(k, t):
        source = src[k, t]
        own = (source < local) | (source == local + me)
        return (t < count[k]) & own

    def copy(k, t):
        return pltpu.make_async_copy(tiles.at[k, t], buf.at[k, t], sems.at[k, t])

    for k in range(comms):
        for t in range(slots):
            pl.when(wanted(k, t))(copy(k, t).start)
    for k in range(comms):
        acc[k] = jnp.zeros(acc.shape[1:], jnp.float32)
        for t in range(slots):

            @pl.when(wanted(k, t))
            def _():
                copy(k, t).wait()
                source = src[k, t]
                block = jnp.where(source < local, source, request[0, me])

                @pl.loop(0, acc.shape[1] // ROWS)
                def _(i):
                    rows = pl.ds(pl.multiple_of(i * ROWS, ROWS), ROWS)
                    acc[k, rows, :] += jnp.dot(
                        buf[k, t, rows, :], feats[block], preferred_element_type=jnp.float32
                    )


def call_own_products(src, count, request, feats, tiles):
    comms, slots, nodes, _ = tiles.shape
    width = feats.shape[2]
    return pl.pallas_call(
        own_products,
        out_shape=jax.ShapeDtypeStruct((comms, nodes, width), jnp.float32),
        in_specs=[SMEM, SMEM, SMEM, VMEM, ANY],
        out_specs=VMEM,
        scratch_shapes=[
            pltpu.VMEM(tiles.shape, tiles.dtype),
            pltpu.SemaphoreType.DMA((comms, slots)),
        ],
        compiler_params=pltpu.CompilerParams(vmem_limit_bytes=LIMIT),
        cost_estimate=pl.CostEstimate(
            flops=3 * 2 * nodes * nodes * width, bytes_accessed=4 * 2**20, transcendentals=0
        ),
        name="own_products",
    )(src, count, request, feats, tiles)


def update(
    src, count, tiles, from1, from2, from3, acc, weight, z_old, dual, target, rho, beta,
    new_z, new_dual, agg, buf, total, zbuf, dbuf, sems, osems,
):
    me = lax.axis_index("comm")
    comms, slots, nodes, _ = tiles.shape
    local = comms
    hidden = weight.shape[1]
    per = nodes // ROWS
    steps = comms * per

    def step_of(k, t):
        source = src[k, t]
        rel = lax.rem(source - local - me + 8, 4)
        live = (t < count[k]) & (source >= local) & (rel > 0)
        return live, rel

    def copy(k, t):
        return pltpu.make_async_copy(tiles.at[k, t], buf.at[k, t], sems.at[k, t])

    def out_copies(i, slot):
        rows = pl.ds(pl.multiple_of(i * ROWS, ROWS), ROWS)
        return (
            pltpu.make_async_copy(zbuf.at[slot], new_z.at[rows, :], osems.at[0, slot]),
            pltpu.make_async_copy(dbuf.at[slot], new_dual.at[rows, :], osems.at[1, slot]),
        )

    for k in range(comms):
        for t in range(slots):
            pl.when(step_of(k, t)[0])(copy(k, t).start)

    @pl.loop(0, steps)
    def _(i):
        k = i // per
        first = i - k * per == 0
        rows = pl.ds(pl.multiple_of((i - k * per) * ROWS, ROWS), ROWS)
        flat = pl.ds(pl.multiple_of(i * ROWS, ROWS), ROWS)
        slot = lax.rem(i, 2)
        total[...] = acc[k, rows, :]
        for t in range(slots):
            live, rel = step_of(k, t)

            @pl.when(live & first)
            def _():
                copy(k, t).wait()

            for r, block in ((1, from1), (2, from2), (3, from3)):

                @pl.when(live & (rel == r))
                def _():
                    total[...] += jnp.dot(
                        buf[k, t, rows, :], block[...], preferred_element_type=jnp.float32
                    )

        part = total[...].astype(jnp.bfloat16)
        agg[flat, :] = part

        @pl.when(i >= 2)
        def _():
            for c in out_copies(i - 2, slot):
                c.wait()

        for h in range(hidden // COLS):
            cols = slice(h * COLS, (h + 1) * COLS)
            r, b = rho[:, cols], beta[:, cols]
            share = b / (r + b)
            pre = jnp.dot(part, weight[:, cols], preferred_element_type=jnp.float32)
            v = pre + dual[flat, cols].astype(jnp.float32) * (1.0 / r)
            gap = jnp.where(
                z_old[flat, cols].astype(jnp.float32) > 0,
                (v - target[flat, cols].astype(jnp.float32)) * share,
                0.0,
            )
            zbuf[slot, :, cols] = (v - gap).astype(jnp.bfloat16)
            dbuf[slot, :, cols] = (r * gap).astype(jnp.bfloat16)
        for c in out_copies(i, slot):
            c.start()

    for i in (steps - 2, steps - 1):
        for c in out_copies(i, i % 2):
            c.wait()


def call_update(src, count, tiles, blocks, acc, weight, z_old, dual, target, rho, beta):
    comms, slots, nodes, _ = tiles.shape
    width, hidden = weight.shape
    flat = comms * nodes
    return pl.pallas_call(
        update,
        out_shape=(
            jax.ShapeDtypeStruct((flat, hidden), jnp.bfloat16),
            jax.ShapeDtypeStruct((flat, hidden), jnp.bfloat16),
            jax.ShapeDtypeStruct((flat, width), jnp.bfloat16),
        ),
        in_specs=[SMEM, SMEM, ANY] + [VMEM] * 10,
        out_specs=(ANY, ANY, VMEM),
        scratch_shapes=[
            pltpu.VMEM(tiles.shape, tiles.dtype),
            pltpu.VMEM((ROWS, width), jnp.float32),
            pltpu.VMEM((2, ROWS, hidden), jnp.bfloat16),
            pltpu.VMEM((2, ROWS, hidden), jnp.bfloat16),
            pltpu.SemaphoreType.DMA((comms, slots)),
            pltpu.SemaphoreType.DMA((2, 2)),
        ],
        compiler_params=pltpu.CompilerParams(vmem_limit_bytes=LIMIT),
        cost_estimate=pl.CostEstimate(
            flops=2 * flat * width * hidden + 3 * 2 * nodes * nodes * width,
            bytes_accessed=12 * 2**20,
            transcendentals=0,
        ),
        name="update",
    )(src, count, tiles, *blocks, acc, weight, z_old, dual, target, rho[None], beta[None])


def reduced(grad, factor):
    width, hidden = grad.shape
    y, z, core = place(lax.axis_index("wide"))
    pick = functools.partial(lax.dynamic_index_in_dim, keepdims=False)
    f32 = lambda x: x.astype(jnp.float32)
    parts = grad.reshape(4, 4, 2, width // 32, hidden)
    held = f32(pick(parts, core, 2)) + f32(along_core(pick(parts, 1 - core, 2)))
    parts = held.astype(jnp.bfloat16)
    held = f32(pick(parts, z, 1))
    for step in (1, 2, 3):
        held = held + f32(along_z(pick(parts, (z + step) % 4, 1), step))
    parts = held.astype(jnp.bfloat16)
    held = f32(pick(parts, y, 0))
    for step in (1, 2, 3):
        held = held + f32(along_y(pick(parts, (y + step) % 4, 0), step))
    mine = held.astype(jnp.bfloat16)
    held = f32(mine)
    for step in (1, 2, 3):
        held = held + f32(along_comm(mine, step))
    return held * factor


def local(feats, tiles, tile_src, tile_count, request, z_old, dual, target, w_rows, rho, beta):
    comms, nodes, width = feats.shape
    hidden = w_rows.shape[1]
    me = lax.axis_index("comm")
    blocks = []
    for rel in (1, 2, 3):
        step = 4 - rel
        asked = along_comm(request, rel)[0, me]
        block = lax.dynamic_index_in_dim(feats, asked, 0, keepdims=False)
        blocks.append(along_comm(block, step))
    acc = call_own_products(tile_src, tile_count, request, feats, tiles)
    weight = lax.all_gather(w_rows, "wide", axis=0, tiled=True)
    flat = lambda x: x.reshape(comms * nodes, hidden)
    new_z, new_dual, agg = call_update(
        tile_src, tile_count, tiles, blocks, acc, weight,
        flat(z_old), flat(dual), flat(target), rho, beta,
    )
    grad = jnp.einsum("nf,nh->fh", agg, new_dual, preferred_element_type=jnp.float32)
    total_nodes = comms * nodes * lax.axis_size("comm") * lax.axis_size("wide")
    grad = reduced(grad.astype(jnp.bfloat16), 1.0 / math.sqrt(total_nodes))
    return new_z.reshape(z_old.shape), new_dual.reshape(z_old.shape), grad


def solution(mesh):
    split = P(("comm", "wide"))
    in_specs = (split,) * 8 + (P("wide"), P(), P())
    out_specs = (split, split, P("wide"))
    return jax.shard_map(local, mesh=mesh, in_specs=in_specs, out_specs=out_specs, check_vma=False)
```

time: 189 us -> 156 us (0.83); the launches traced: 186 us -> 156 us
  blocking collectives: 63.3 us -> 0 us
  waiting for transfers between devices: 48.8 us -> 67.7 us
  starting transfers between devices: 5.12 us -> 23.1 us
  Pallas kernels: 0 us -> 14.9 us
  matrix products: 18.4 us -> 4.59 us
  other arithmetic: 11.6 us -> 1.13 us
  local copies, waits for them, and re-layouts: 16.5 us -> 24.3 us
  loops' own time: 3.95 us -> 0 us
  between operations: 18.1 us -> 20 us
    ppermute x0 -> x16, waiting for transfers between devices: none -> 67 us  [shifted(): return lax.ppermute(x, axis, [(i, to(i)) for i in range(size)])]
    all_to_all x2 -> x0, blocking collectives: 51.1 us -> none  [the longest x1 41.7 us: summed_on_arrival(): lax.all_to_all(tiles, axis, split_axis=0, concat_axis=0, tiled=True)]
    all_to_all x1 -> x0, waiting for transfers between devices: 48.1 us -> none  [local(): lax.all_to_all(outgoing, 'comm', split_axis=0, concat_axis=0, tiled=True)]
    ppermute x0 -> x16, starting transfers between devices: none -> 23 us  [shifted(): return lax.ppermute(x, axis, [(i, to(i)) for i in range(size)])]
    unnamed x18 -> x28, local copies, waits for them, and re-layouts: 0.04 us -> 18.3 us
    pallas_call x0 -> x2, Pallas kernels: none -> 14.9 us  [the longest x1 10.5 us: call_update(): pl.pallas_call(update, out_shape=(jax.ShapeDtypeStruct((flat, hidden), jn...]
    dot_general x5 -> x1, matrix products: 18.4 us -> 4.59 us  [local(): jnp.einsum('nf,nh->fh', agg, new_dual, preferred_element_type=jnp.float32)]
    all_gather x1 -> x0, blocking collectives: 12.2 us -> none  [total_of_pieces(): tiles = lax.all_gather(shard, axis).astype(jnp.float32)]
  transfers between devices with their start and end apart: 2 -> 17, of which waited for: 1 -> 13; matrix products, arithmetic and copies ran while one was open for 15% -> 4% of each run, Pallas kernels for 0% -> 3%
where the time goes in v1:
time: 156 us
  waiting for transfers between devices  67.7 us (43%)
  local copies, waits for them, and re-layouts  24.3 us (16%)
  starting transfers between devices  23.1 us (15%)
  between operations  20 us (13%)
  Pallas kernels  14.9 us (10%)
  matrix products  4.59 us (3%)
    ppermute x16, waiting for transfers between devices, shifted(): return lax.ppermute(x, axis, [(i, to(i)) for i in range(size)])  67 us
    ppermute x16, starting transfers between devices, shifted(): return lax.ppermute(x, axis, [(i, to(i)) for i in range(size)])  23 us
    unnamed x28, local copies, waits for them, and re-layouts  18.3 us
    pallas_call x1, Pallas kernels, call_update(): pl.pallas_call(update, out_shape=(jax.ShapeDtypeStruct((flat, hidden), jn...  10.5 us
    dot_general x1, matrix products, local(): jnp.einsum('nf,nh->fh', agg, new_dual, preferred_element_type=jnp.float32)  4.59 us
    pallas_call x1, Pallas kernels, call_own_products(): pl.pallas_call(own_products, out_shape=jax.ShapeDtypeStruct((comms, nodes...  4.42 us
    squeeze x1, local copies, waits for them, and re-layouts, local(): block = lax.dynamic_index_in_dim(feats, asked, 0, keepdims=False)  4.03 us
  transfers between devices with their start and end apart: 17, of which 13 were waited for; matrix products, arithmetic and copies ran while one was open for 4% of the time, Pallas kernels for 3%

profile of v1, /device:TPU:0, one launch (start us, length us, event | category | flops | bytes accessed | tf_op | source)
XLA Modules:
  0.0 155.7 jit_solution(12312031851814239343)
XLA Ops:
  7.9 2.9 %collective-permute-start.4 = (s32[1,4]{1,0:T(1,128)}, s32[1,4]{1,0:T(1,128)S(1)}, u32[]{:S(2)}, u32[]{:S(2)}) collective-permute-start(s32[1,4]{1,0:T(1,128)} %request.1), channel_id=1, source_target_pairs={{0,96},{32,0},{64,32},{96,64},{1,97},{33,1},{65,33},{97,65},{2,98}... | collective-permute-start | bytes 56 | tf_op jit(solution)/shard_map/ppermute | solution.py:21
  14.4 1.6 %collective-permute-done.2 = s32[1,4]{1,0:T(1,128)S(1)} collective-permute-done((s32[1,4]{1,0:T(1,128)}, s32[1,4]{1,0:T(1,128)S(1)}, u32[]{:S(2)}, u32[]{:S(2)}) %collective-permute-start.2) | collective-permute-done | bytes 48 | tf_op jit(solution)/shard_map/ppermute | solution.py:21
  21.7 4.0 %dynamic-slice_bitcast_fusion = (bf16[768,768]{1,0:T(8,128)(2,1)}, bf16[768,768]{1,0:T(8,128)(2,1)}, bf16[768,768]{1,0:T(8,128)(2,1)}) fusion(bf16[2,768,768]{2,1,0:T(8,128)(2,1)} %feats.1, s32[]{:T(128)S(6)} %select_n.93, s32[]{:T(128)S(6)} %select_n.92, s32[]{:T(128)S(6)} %select_n.91), kind=kLoop, calls=%fused_computation.3 | loop fusion | bytes 7077900 | tf_op jit(solution)/shard_map/jit(dynamic_index_in_dim)/squeeze | solution.py:242
  25.8 1.6 %collective-permute-start.1 = (bf16[768,768]{1,0:T(8,128)(2,1)}, bf16[768,768]{1,0:T(8,128)(2,1)S(1)}, u32[]{:S(2)}, u32[]{:S(2)}) collective-permute-start(bf16[768,768]{1,0:T(8,128)(2,1)} %get-tuple-element.11), channel_id=1, source_target_pairs={{0,96},{32,0},{64,32},{96,64},{1,97},{33,1},{65,33},{97,65},{2,98}... | collective-permute-start | bytes 3538952 | tf_op jit(solution)/shard_map/ppermute | solution.py:21
  28.2 3.0 %copy-done = bf16[2,3,768,768]{3,2,1,0:T(8,128)(2,1)S(1)} copy-done((bf16[2,3,768,768]{3,2,1,0:T(8,128)(2,1)S(1)}, bf16[2,3,768,768]{3,2,1,0:T(8,128)(2,1)}, u32[]{:S(2)}) %copy-start) | copy-done | bytes 7077912
  31.9 4.4 %own_products.1.acc = f32[2,768,768]{2,1,0:T(8,128)S(1)} custom-call(s32[2,3]{1,0:T(2,128)S(1)} %copy-done.11, s32[2]{0:T(128)S(1)} %copy-done.12, s32[1,4]{1,0:T(1,128)S(1)} %copy-done.13, bf16[2,768,768]{2,1,0:T(8,128)(2,1)S(1)} %copy-done.4, bf16[2,3,768,768]{3,2,1,0:T(8,128)(2,1)S(1)} %copy-done), custom_call_target="tpu_custom_call" | custom-call | flops 2717908992 | bytes 4194304 | tf_op jit(solution)/shard_map/own_products/pallas_call | solution.py:81
  36.4 2.1 %copy-done.2 = f32[2,768,768]{2,1,0:T(8,128)} copy-done((f32[2,768,768]{2,1,0:T(8,128)}, f32[2,768,768]{2,1,0:T(8,128)S(1)}, u32[]{:S(2)}) %copy-start.2) | copy-done | bytes 4718616
  38.5 38.5 %collective-permute-done.1.from1 = bf16[768,768]{1,0:T(8,128)(2,1)S(1)} collective-permute-done((bf16[768,768]{1,0:T(8,128)(2,1)}, bf16[768,768]{1,0:T(8,128)(2,1)S(1)}, u32[]{:S(2)}, u32[]{:S(2)}) %collective-permute-start.1) | collective-permute-done | bytes 1179680 | tf_op jit(solution)/shard_map/ppermute | solution.py:21
  77.0 3.7 %collective-permute-done.5.from3 = bf16[768,768]{1,0:T(8,128)(2,1)} collective-permute-done((bf16[768,768]{1,0:T(8,128)(2,1)}, bf16[768,768]{1,0:T(8,128)(2,1)}, u32[]{:S(2)}, u32[]{:S(2)}) %collective-permute-start.5) | collective-permute-done | bytes 1179680 | tf_op jit(solution)/shard_map/ppermute | solution.py:21
  80.7 3.0 %copy-done.1 = bf16[2,3,768,768]{3,2,1,0:T(8,128)(2,1)S(1)} copy-done((bf16[2,3,768,768]{3,2,1,0:T(8,128)(2,1)S(1)}, bf16[2,3,768,768]{3,2,1,0:T(8,128)(2,1)}, u32[]{:S(2)}) %copy-start.1) | copy-done | bytes 7077912
  83.8 2.3 %copy-done.3 = f32[2,768,768]{2,1,0:T(8,128)S(1)} copy-done((f32[2,768,768]{2,1,0:T(8,128)S(1)}, f32[2,768,768]{2,1,0:T(8,128)}, u32[]{:S(2)}) %copy-start.3) | copy-done | bytes 4718616
  86.1 1.9 %copy-done.5 = bf16[2,768,1024]{2,1,0:T(8,128)(2,1)S(1)} copy-done((bf16[2,768,1024]{2,1,0:T(8,128)(2,1)S(1)}, bf16[2,768,1024]{2,1,0:T(8,128)(2,1)}, u32[]{:S(2)}) %copy-start.5) | copy-done | bytes 3145752
  88.0 1.9 %copy-done.6 = bf16[2,768,1024]{2,1,0:T(8,128)(2,1)S(1)} copy-done((bf16[2,768,1024]{2,1,0:T(8,128)(2,1)S(1)}, bf16[2,768,1024]{2,1,0:T(8,128)(2,1)}, u32[]{:S(2)}) %copy-start.6) | copy-done | bytes 3145752
  89.9 1.9 %copy-done.7 = bf16[2,768,1024]{2,1,0:T(8,128)(2,1)S(1)} copy-done((bf16[2,768,1024]{2,1,0:T(8,128)(2,1)S(1)}, bf16[2,768,1024]{2,1,0:T(8,128)(2,1)}, u32[]{:S(2)}) %copy-start.7) | copy-done | bytes 3145752
  93.2 10.5 %update.1 = (bf16[1536,1024]{1,0:T(8,128)(2,1)}, bf16[1536,1024]{1,0:T(8,128)(2,1)}, bf16[1536,768]{1,0:T(8,128)(2,1)S(1)}) custom-call(s32[2,3]{1,0:T(2,128)S(1)} %copy-done.11, s32[2]{0:T(128)S(1)} %copy-done.12, bf16[2,3,768,768]{3,2,1,0:T(8,128)(2,1)S(1)} %copy-done.1, bf16[768,768]{1,0:T(8,128)(2,1)S(1)} %collective-permute-done.1.from1, ...), custom_call_target="tpu_custom_call" | custom-call | flops 5133828096 | bytes 12582912 | tf_op jit(solution)/shard_map/update/pallas_call | solution.py:185
  103.7 4.6 %convolution_convert_fusion = bf16[768,1024]{1,0:T(8,128)(2,1)S(1)} fusion(bf16[1536,768]{1,0:T(8,128)(2,1)S(1)} %get-tuple-element.8, bf16[1536,1024]{1,0:T(8,128)(2,1)} %get-tuple-element.7), kind=kOutput, calls=%fused_computation | convolution fusion | flops 2416705536 | bytes 7077888 | tf_op jit(solution)/shard_map/nf,nh->fh/dot_general | solution.py:251
  108.5 1.9 %collective-permute-start.6 = (bf16[4,4,24,1024]{3,2,0,1:T(8,128)(2,1)S(1)}, bf16[4,4,24,1024]{3,2,0,1:T(8,128)(2,1)S(1)}, u32[]{:S(2)}, u32[]{:S(2)}) collective-permute-start(bf16[4,4,24,1024]{3,2,0,1:T(8,128)(2,1)S(1)} %bitcast.51), channel_id=1, source_target_pairs={{0,1},{1,0},{2,3},{3,2},{4,5},{5,4},{6,7},{7,6},{8,9},{9,8},{10,11... | collective-permute-start | bytes 2359304 | tf_op jit(solution)/shard_map/ppermute | solution.py:21
  110.4 1.9 %collective-permute-done.6 = bf16[4,4,24,1024]{3,2,0,1:T(8,128)(2,1)S(1)} collective-permute-done((bf16[4,4,24,1024]{3,2,0,1:T(8,128)(2,1)S(1)}, bf16[4,4,24,1024]{3,2,0,1:T(8,128)(2,1)S(1)}, u32[]{:S(2)}, u32[]{:S(2)}) %collective-permute-start.6) | collective-permute-done | bytes 786464 | tf_op jit(solution)/shard_map/ppermute | solution.py:21
  112.7 5.8 %collective-permute-start.9 = (bf16[4,24,1024]{2,1,0:T(8,128)(2,1)S(1)}, bf16[4,24,1024]{2,1,0:T(8,128)(2,1)S(1)}, u32[]{:S(2)}, u32[]{:S(2)}) collective-permute-start(bf16[4,24,1024]{2,1,0:T(8,128)(2,1)S(1)} %get-tuple-element.15), channel_id=1, source_target_pairs={{0,6},{1,7},{2,0},{3,1},{4,2},{5,3},{6,4},{7,5},{8,14},{9,15},{10,... | collective-permute-start | bytes 589832 | tf_op jit(solution)/shard_map/ppermute | solution.py:21
  119.4 7.9 %collective-permute-done.9 = bf16[4,24,1024]{2,1,0:T(8,128)(2,1)S(1)} collective-permute-done((bf16[4,24,1024]{2,1,0:T(8,128)(2,1)S(1)}, bf16[4,24,1024]{2,1,0:T(8,128)(2,1)S(1)}, u32[]{:S(2)}, u32[]{:S(2)}) %collective-permute-start.9) | collective-permute-done | bytes 196640 | tf_op jit(solution)/shard_map/ppermute | solution.py:21
  127.8 3.0 %collective-permute-done.7 = bf16[4,24,1024]{2,1,0:T(8,128)(2,1)S(1)} collective-permute-done((bf16[4,24,1024]{2,1,0:T(8,128)(2,1)S(1)}, bf16[4,24,1024]{2,1,0:T(8,128)(2,1)S(1)}, u32[]{:S(2)}, u32[]{:S(2)}) %collective-permute-start.7) | collective-permute-done | bytes 196640 | tf_op jit(solution)/shard_map/ppermute | solution.py:21
  130.9 3.5 %collective-permute-start.12 = (bf16[24,1024]{1,0:T(8,128)(2,1)S(1)}, bf16[24,1024]{1,0:T(8,128)(2,1)S(1)}, u32[]{:S(2)}, u32[]{:S(2)}) collective-permute-start(bf16[24,1024]{1,0:T(8,128)(2,1)S(1)} %get-tuple-element.18), channel_id=1, source_target_pairs={{0,24},{1,25},{2,26},{3,27},{4,28},{5,29},{6,30},{7,31},{8,0},{9,1... | collective-permute-start | bytes 147464 | tf_op jit(solution)/shard_map/ppermute | solution.py:21
  136.2 3.9 %collective-permute-done.11 = bf16[24,1024]{1,0:T(8,128)(2,1)S(1)} collective-permute-done((bf16[24,1024]{1,0:T(8,128)(2,1)S(1)}, bf16[24,1024]{1,0:T(8,128)(2,1)S(1)}, u32[]{:S(2)}, u32[]{:S(2)}) %collective-permute-start.11) | collective-permute-done | bytes 49184 | tf_op jit(solution)/shard_map/ppermute | solution.py:21
  144.5 2.9 %collective-permute-done.14 = bf16[24,1024]{1,0:T(8,128)(2,1)S(1)} collective-permute-done((bf16[24,1024]{1,0:T(8,128)(2,1)S(1)}, bf16[24,1024]{1,0:T(8,128)(2,1)S(1)}, u32[]{:S(2)}, u32[]{:S(2)}) %collective-permute-start.14) | collective-permute-done | bytes 49184 | tf_op jit(solution)/shard_map/ppermute | solution.py:21
  (54 shorter events, 16.8 us)
Async XLA Ops:
  7.2 73.6 %all-gather.2.cloned.1.call-start = ((), (), s32[]{:S(2)}) async-start(), calls=%async_computation | async-start | bytes 1622016 | tf_op jit(solution)/shard_map/all_gather | solution.py:245
  7.9 4.6 %collective-permute-start.4 = (s32[1,4]{1,0:T(1,128)}, s32[1,4]{1,0:T(1,128)S(1)}, u32[]{:S(2)}, u32[]{:S(2)}) collective-permute-start(s32[1,4]{1,0:T(1,128)} %request.1), channel_id=1, source_target_pairs={{0,96},{32,0},{64,32},{96,64},{1,97},{33,1},{65,33},{97,65},{2,98}... | collective-permute-start | bytes 56 | tf_op jit(solution)/shard_map/ppermute | solution.py:21
  10.8 5.2 %collective-permute-start.2 = (s32[1,4]{1,0:T(1,128)}, s32[1,4]{1,0:T(1,128)S(1)}, u32[]{:S(2)}, u32[]{:S(2)}) collective-permute-start(s32[1,4]{1,0:T(1,128)} %request.1), channel_id=1, source_target_pairs={{0,64},{32,96},{64,0},{96,32},{1,65},{33,97},{65,1},{97,33},{2,66}... | collective-permute-start | bytes 56 | tf_op jit(solution)/shard_map/ppermute | solution.py:21
  11.6 6.3 %collective-permute-start = (s32[1,4]{1,0:T(1,128)}, s32[1,4]{1,0:T(1,128)S(1)}, u32[]{:S(2)}, u32[]{:S(2)}) collective-permute-start(s32[1,4]{1,0:T(1,128)} %request.1), channel_id=1, source_target_pairs={{0,32},{32,64},{64,96},{96,0},{1,33},{33,65},{65,97},{97,1},{2,34}... | collective-permute-start | bytes 56 | tf_op jit(solution)/shard_map/ppermute | solution.py:21
  21.7 6.5 %copy-start.4 = (bf16[2,768,768]{2,1,0:T(8,128)(2,1)S(1)}, bf16[2,768,768]{2,1,0:T(8,128)(2,1)}, u32[]{:S(2)}) copy-start(bf16[2,768,768]{2,1,0:T(8,128)(2,1)} %feats.1) | copy-start | bytes 7077892
  21.7 6.5 %copy-start.11 = (s32[2,3]{1,0:T(2,128)S(1)}, s32[2,3]{1,0:T(2,128)}, u32[]{:S(2)}) copy-start(s32[2,3]{1,0:T(2,128)} %src.3) | copy-start | bytes 76
  21.7 6.5 %copy-start.12 = (s32[2]{0:T(128)S(1)}, s32[2]{0:T(128)}, u32[]{:S(2)}) copy-start(s32[2]{0:T(128)} %count.3) | copy-start | bytes 28
  25.8 51.3 %collective-permute-start.1 = (bf16[768,768]{1,0:T(8,128)(2,1)}, bf16[768,768]{1,0:T(8,128)(2,1)S(1)}, u32[]{:S(2)}, u32[]{:S(2)}) collective-permute-start(bf16[768,768]{1,0:T(8,128)(2,1)} %get-tuple-element.11), channel_id=1, source_target_pairs={{0,96},{32,0},{64,32},{96,64},{1,97},{33,1},{65,33},{97,65},{2,98}... | collective-permute-start | bytes 3538952 | tf_op jit(solution)/shard_map/ppermute | solution.py:21
  27.4 49.7 %collective-permute-start.3 = (bf16[768,768]{1,0:T(8,128)(2,1)}, bf16[768,768]{1,0:T(8,128)(2,1)}, u32[]{:S(2)}, u32[]{:S(2)}) collective-permute-start(bf16[768,768]{1,0:T(8,128)(2,1)} %get-tuple-element.10), channel_id=1, source_target_pairs={{0,64},{32,96},{64,0},{96,32},{1,65},{33,97},{65,1},{97,33},{2,66}... | collective-permute-start | bytes 3538952 | tf_op jit(solution)/shard_map/ppermute | solution.py:21
  28.0 52.7 %collective-permute-start.5 = (bf16[768,768]{1,0:T(8,128)(2,1)}, bf16[768,768]{1,0:T(8,128)(2,1)}, u32[]{:S(2)}, u32[]{:S(2)}) collective-permute-start(bf16[768,768]{1,0:T(8,128)(2,1)} %get-tuple-element.9), channel_id=1, source_target_pairs={{0,32},{32,64},{64,96},{96,0},{1,33},{33,65},{65,97},{97,1},{2,34}... | collective-permute-start | bytes 3538952 | tf_op jit(solution)/shard_map/ppermute | solution.py:21
  28.2 3.0 %copy-start = (bf16[2,3,768,768]{3,2,1,0:T(8,128)(2,1)S(1)}, bf16[2,3,768,768]{3,2,1,0:T(8,128)(2,1)}, u32[]{:S(2)}) copy-start(bf16[2,3,768,768]{3,2,1,0:T(8,128)(2,1)} %tiles.3) | copy-start | bytes 21233668
  31.9 48.8 %copy-start.9 = (f32[1024]{0:T(1024)S(1)}, f32[1024]{0:T(1024)}, u32[]{:S(2)}) copy-start(f32[1024]{0:T(1024)} %param.20) | copy-start | bytes 12292
  31.9 48.8 %copy-start.10 = (f32[1024]{0:T(1024)S(1)}, f32[1024]{0:T(1024)}, u32[]{:S(2)}) copy-start(f32[1024]{0:T(1024)} %param.21) | copy-start | bytes 12292
  80.7 3.0 %copy-start.1 = (bf16[2,3,768,768]{3,2,1,0:T(8,128)(2,1)S(1)}, bf16[2,3,768,768]{3,2,1,0:T(8,128)(2,1)}, u32[]{:S(2)}) copy-start(bf16[2,3,768,768]{3,2,1,0:T(8,128)(2,1)} %tiles.3) | copy-start | bytes 21233668
  108.5 3.8 %collective-permute-start.6 = (bf16[4,4,24,1024]{3,2,0,1:T(8,128)(2,1)S(1)}, bf16[4,4,24,1024]{3,2,0,1:T(8,128)(2,1)S(1)}, u32[]{:S(2)}, u32[]{:S(2)}) collective-permute-start(bf16[4,4,24,1024]{3,2,0,1:T(8,128)(2,1)S(1)} %bitcast.51), channel_id=1, source_target_pairs={{0,1},{1,0},{2,3},{3,2},{4,5},{5,4},{6,7},{7,6},{8,9},{9,8},{10,11... | collective-permute-start | bytes 2359304 | tf_op jit(solution)/shard_map/ppermute | solution.py:21
  112.7 14.7 %collective-permute-start.9 = (bf16[4,24,1024]{2,1,0:T(8,128)(2,1)S(1)}, bf16[4,24,1024]{2,1,0:T(8,128)(2,1)S(1)}, u32[]{:S(2)}, u32[]{:S(2)}) collective-permute-start(bf16[4,24,1024]{2,1,0:T(8,128)(2,1)S(1)} %get-tuple-element.15), channel_id=1, source_target_pairs={{0,6},{1,7},{2,0},{3,1},{4,2},{5,3},{6,4},{7,5},{8,14},{9,15},{10,... | collective-permute-start | bytes 589832 | tf_op jit(solution)/shard_map/ppermute | solution.py:21
  118.5 9.3 %collective-permute-start.8 = (bf16[4,24,1024]{2,1,0:T(8,128)(2,1)S(1)}, bf16[4,24,1024]{2,1,0:T(8,128)(2,1)S(1)}, u32[]{:S(2)}, u32[]{:S(2)}) collective-permute-start(bf16[4,24,1024]{2,1,0:T(8,128)(2,1)S(1)} %get-tuple-element.16), channel_id=1, source_target_pairs={{0,4},{1,5},{2,6},{3,7},{4,0},{5,1},{6,2},{7,3},{8,12},{9,13},{10,... | collective-permute-start | bytes 589832 | tf_op jit(solution)/shard_map/ppermute | solution.py:21
  118.7 12.0 %collective-permute-start.7 = (bf16[4,24,1024]{2,1,0:T(8,128)(2,1)S(1)}, bf16[4,24,1024]{2,1,0:T(8,128)(2,1)S(1)}, u32[]{:S(2)}, u32[]{:S(2)}) collective-permute-start(bf16[4,24,1024]{2,1,0:T(8,128)(2,1)S(1)} %get-tuple-element.14), channel_id=1, source_target_pairs={{0,2},{1,3},{2,4},{3,5},{4,6},{5,7},{6,0},{7,1},{8,10},{9,11},{10,... | collective-permute-start | bytes 589832 | tf_op jit(solution)/shard_map/ppermute | solution.py:21
  130.9 5.3 %collective-permute-start.12 = (bf16[24,1024]{1,0:T(8,128)(2,1)S(1)}, bf16[24,1024]{1,0:T(8,128)(2,1)S(1)}, u32[]{:S(2)}, u32[]{:S(2)}) collective-permute-start(bf16[24,1024]{1,0:T(8,128)(2,1)S(1)} %get-tuple-element.18), channel_id=1, source_target_pairs={{0,24},{1,25},{2,26},{3,27},{4,28},{5,29},{6,30},{7,31},{8,0},{9,1... | collective-permute-start | bytes 147464 | tf_op jit(solution)/shard_map/ppermute | solution.py:21
  134.4 5.6 %collective-permute-start.11 = (bf16[24,1024]{1,0:T(8,128)(2,1)S(1)}, bf16[24,1024]{1,0:T(8,128)(2,1)S(1)}, u32[]{:S(2)}, u32[]{:S(2)}) collective-permute-start(bf16[24,1024]{1,0:T(8,128)(2,1)S(1)} %get-tuple-element.19), channel_id=1, source_target_pairs={{0,16},{1,17},{2,18},{3,19},{4,20},{5,21},{6,22},{7,23},{8,24},{9,... | collective-permute-start | bytes 147464 | tf_op jit(solution)/shard_map/ppermute | solution.py:21
  134.4 5.8 %collective-permute-start.10 = (bf16[24,1024]{1,0:T(8,128)(2,1)S(1)}, bf16[24,1024]{1,0:T(8,128)(2,1)S(1)}, u32[]{:S(2)}, u32[]{:S(2)}) collective-permute-start(bf16[24,1024]{1,0:T(8,128)(2,1)S(1)} %get-tuple-element.17), channel_id=1, source_target_pairs={{0,8},{1,9},{2,10},{3,11},{4,12},{5,13},{6,14},{7,15},{8,16},{9,17... | collective-permute-start | bytes 147464 | tf_op jit(solution)/shard_map/ppermute | solution.py:21
  140.3 4.2 %collective-permute-start.15 = (bf16[24,1024]{1,0:T(8,128)(2,1)S(1)}, bf16[24,1024]{1,0:T(8,128)(2,1)S(1)}, u32[]{:S(2)}, u32[]{:S(2)}) collective-permute-start(bf16[24,1024]{1,0:T(8,128)(2,1)S(1)} %fusion.6), channel_id=1, source_target_pairs={{0,96},{32,0},{64,32},{96,64},{1,97},{33,1},{65,33},{97,65},{2,98}... | collective-permute-start | bytes 147464 | tf_op jit(solution)/shard_map/ppermute | solution.py:21
  141.8 5.6 %collective-permute-start.14 = (bf16[24,1024]{1,0:T(8,128)(2,1)S(1)}, bf16[24,1024]{1,0:T(8,128)(2,1)S(1)}, u32[]{:S(2)}, u32[]{:S(2)}) collective-permute-start(bf16[24,1024]{1,0:T(8,128)(2,1)S(1)} %fusion.6), channel_id=1, source_target_pairs={{0,64},{32,96},{64,0},{96,32},{1,65},{33,97},{65,1},{97,33},{2,66}... | collective-permute-start | bytes 147464 | tf_op jit(solution)/shard_map/ppermute | solution.py:21
  142.9 5.3 %collective-permute-start.13 = (bf16[24,1024]{1,0:T(8,128)(2,1)S(1)}, bf16[24,1024]{1,0:T(8,128)(2,1)S(1)}, u32[]{:S(2)}, u32[]{:S(2)}) collective-permute-start(bf16[24,1024]{1,0:T(8,128)(2,1)S(1)} %fusion.6), channel_id=1, source_target_pairs={{0,32},{32,64},{64,96},{96,0},{1,33},{33,65},{65,97},{97,1},{2,34}... | collective-permute-start | bytes 147464 | tf_op jit(solution)/shard_map/ppermute | solution.py:21
  (7 other events, 12.2 us)
Sparse Core Ops, SparseCore 0:
  10.2 45.8 all-gather.1

commit v2 on v1

v2 whole, which is shorter than its diff:
```python
import functools
import math

import jax
import jax.numpy as jnp
from jax import lax
from jax.experimental import pallas as pl
from jax.experimental.pallas import tpu as pltpu
from jax.sharding import PartitionSpec as P

ROWS = 256
COLS = 256
FEATS = 384
CUTS = (512, 256, 512)
SMALL = pl.CostEstimate(flops=2**20, bytes_accessed=2**16, transcendentals=0)
SMEM = pl.BlockSpec(memory_space=pltpu.SMEM)
VMEM = pl.BlockSpec(memory_space=pltpu.VMEM)
HBM = pl.BlockSpec(memory_space=pltpu.HBM)


def shifted(x, axis, to):
    size = lax.axis_size(axis)
    return lax.ppermute(x, axis, [(i, to(i)) for i in range(size)])


def place(w):
    return w // 8, w // 2 % 4, w % 2


def along_comm(x, step):
    return shifted(x, "comm", lambda i: (i + step) % 4)


def along_core(x):
    return shifted(x, "wide", lambda w: w ^ 1)


def along_z(x, step):
    return shifted(x, "wide", lambda w: w // 8 * 8 + (w // 2 % 4 + step) % 4 * 2 + w % 2)


def along_y(x, step):
    return shifted(x, "wide", lambda w: (w // 8 + step) % 4 * 8 + w % 8)


def in_hbm(x):
    return pltpu.with_memory_space_constraint(x, pltpu.HBM)


def me_on_comm():
    return lax.axis_index("comm")


def choose(ask1, ask2, ask3, feats, *refs):
    outs, sems = refs[:-1], refs[-1]
    me = me_on_comm()
    copies = []
    for n, ask in enumerate((ask1, ask2, ask3)):
        asked, cut = ask[0, me], CUTS[n]
        for part, cols in enumerate((slice(0, cut), slice(cut, feats.shape[2]))):
            copies.append(
                pltpu.make_async_copy(
                    feats.at[asked, :, cols], outs[2 * n + part], sems.at[2 * n + part]
                )
            )
    for c in copies:
        c.start()
    for c in copies:
        c.wait()


def call_choose(asks, feats):
    nodes, width = feats.shape[1:]
    shapes = [
        jax.ShapeDtypeStruct((nodes, cols), feats.dtype)
        for cut in CUTS
        for cols in (cut, width - cut)
    ]
    return pl.pallas_call(
        choose,
        out_shape=shapes,
        in_specs=[SMEM] * 3 + [HBM],
        out_specs=[VMEM] * len(shapes),
        scratch_shapes=[pltpu.SemaphoreType.DMA((len(shapes),))],
        compiler_params=pltpu.CompilerParams(vmem_limit_bytes=2**20),
        cost_estimate=SMALL,
        name="choose",
    )(*asks, in_hbm(feats))


def own_products(
    src, count, request, feats, tiles, z_old, dual, target,
    acc, far, zs, ds, ts, buf, sems, fsems, xsems,
):
    me = me_on_comm()
    comms, slots = tiles.shape[0], tiles.shape[1]
    local = feats.shape[0]

    def live(k, t):
        return t < count[k]

    def own(k, t):
        source = src[k, t]
        return (source < local) | (source == local + me)

    def near_copy(k, t):
        return pltpu.make_async_copy(tiles.at[k, t], buf.at[k, t], sems.at[k, t])

    def far_copy(k, t):
        return pltpu.make_async_copy(tiles.at[k, t], far.at[k, t], fsems.at[k, t])

    staged = [
        pltpu.make_async_copy(a, b, xsems.at[n])
        for n, (a, b) in enumerate(((z_old, zs), (dual, ds), (target, ts)))
    ]
    for k in range(comms):
        for t in range(slots):
            pl.when(live(k, t) & own(k, t))(near_copy(k, t).start)
    for k in range(comms):
        for t in range(slots):
            pl.when(live(k, t) & ~own(k, t))(far_copy(k, t).start)
    for c in staged:
        c.start()
    for k in range(comms):
        acc[k] = jnp.zeros(acc.shape[1:], jnp.float32)
        for t in range(slots):

            @pl.when(live(k, t) & own(k, t))
            def _():
                near_copy(k, t).wait()
                source = src[k, t]
                block = jnp.where(source < local, source, request[0, me])

                @pl.loop(0, acc.shape[1] // ROWS)
                def _(i):
                    rows = pl.ds(pl.multiple_of(i * ROWS, ROWS), ROWS)
                    acc[k, rows, :] += jnp.dot(
                        buf[k, t, rows, :], feats[block], preferred_element_type=jnp.float32
                    )

    for k in range(comms):
        for t in range(slots):
            pl.when(live(k, t) & ~own(k, t))(far_copy(k, t).wait)
    for c in staged:
        c.wait()


def call_own_products(src, count, request, feats, tiles, z_old, dual, target):
    comms, slots, nodes, _ = tiles.shape
    width = feats.shape[2]
    like = lambda a: jax.ShapeDtypeStruct(a.shape, a.dtype)
    return pl.pallas_call(
        own_products,
        out_shape=(
            jax.ShapeDtypeStruct((comms, nodes, width), jnp.float32),
            like(tiles), like(z_old), like(dual), like(target),
        ),
        in_specs=[SMEM, SMEM, SMEM, VMEM] + [HBM] * 4,
        out_specs=(VMEM,) * 5,
        scratch_shapes=[
            pltpu.VMEM(tiles.shape, tiles.dtype),
            pltpu.SemaphoreType.DMA((comms, slots)),
            pltpu.SemaphoreType.DMA((comms, slots)),
            pltpu.SemaphoreType.DMA((3,)),
        ],
        compiler_params=pltpu.CompilerParams(vmem_limit_bytes=10 * 2**20),
        cost_estimate=SMALL,
        name="own_products",
    )(src, count, request, feats, *map(in_hbm, (tiles, z_old, dual, target)))


def relation(src, count, k, t, local):
    rel = lax.rem(src[k, t] - local - me_on_comm() + 8, 4)
    return (t < count[k]) & (src[k, t] >= local) & (rel > 0), rel


def head_products(src, count, far, head1, head2, head3, before, acc):
    comms, slots, nodes, _ = far.shape
    for k in range(comms):
        for t in range(slots):
            live, rel = relation(src, count, k, t, comms)
            for r, (block, cut) in enumerate(zip((head1, head2, head3), CUTS), 1):

                @pl.when(live & (rel == r))
                def _():
                    @pl.loop(0, nodes // ROWS)
                    def _(i):
                        rows = pl.ds(pl.multiple_of(i * ROWS, ROWS), ROWS)
                        acc[k, rows, :cut] += jnp.dot(
                            far[k, t, rows, :], block[...], preferred_element_type=jnp.float32
                        )


def call_head_products(src, count, far, heads, acc):
    return pl.pallas_call(
        head_products,
        out_shape=jax.ShapeDtypeStruct(acc.shape, acc.dtype),
        in_specs=[SMEM, SMEM] + [VMEM] * 5,
        out_specs=VMEM,
        input_output_aliases={6: 0},
        compiler_params=pltpu.CompilerParams(vmem_limit_bytes=4 * 2**20),
        cost_estimate=SMALL,
        name="head_products",
    )(src, count, far, *heads, acc)


def update(
    src, count, far, from1, from2, from3, acc, weight, z_old, dual, target, rho, beta,
    new_z, new_dual, keep, send, agg, total, zbuf, dbuf, osems,
):
    core = my_core()
    comms, slots, nodes, _ = far.shape
    width, hidden = weight.shape
    per = nodes // ROWS
    steps = comms * per

    def out_copies(i):
        rows = pl.ds(pl.multiple_of(i * ROWS, ROWS), ROWS)
        return (
            pltpu.make_async_copy(zbuf.at[rows, :], new_z.at[rows, :], osems.at[0, i]),
            pltpu.make_async_copy(dbuf.at[rows, :], new_dual.at[rows, :], osems.at[1, i]),
        )

    @pl.loop(0, steps)
    def _(i):
        k = i // per
        rows = pl.ds(pl.multiple_of((i - k * per) * ROWS, ROWS), ROWS)
        flat = pl.ds(pl.multiple_of(i * ROWS, ROWS), ROWS)
        total[...] = acc[k, rows, :]
        for t in range(slots):
            live, rel = relation(src, count, k, t, comms)
            for r, (block, cut) in enumerate(zip((from1, from2, from3), CUTS), 1):

                @pl.when(live & (rel == r))
                def _():
                    total[:, cut:] += jnp.dot(
                        far[k, t, rows, :], block[...], preferred_element_type=jnp.float32
                    )

        part = total[...].astype(jnp.bfloat16)
        agg[flat, :] = part
        for h in range(hidden // COLS):
            cols = slice(h * COLS, (h + 1) * COLS)
            r, b = rho[:, cols], beta[:, cols]
            share = b / (r + b)
            pre = jnp.dot(part, weight[:, cols], preferred_element_type=jnp.float32)
            v = pre + dual[flat, cols].astype(jnp.float32) * (1.0 / r)
            gap = jnp.where(
                z_old[flat, cols].astype(jnp.float32) > 0,
                (v - target[flat, cols].astype(jnp.float32)) * share,
                0.0,
            )
            zbuf[flat, cols] = (v - gap).astype(jnp.bfloat16)
            dbuf[flat, cols] = (r * gap).astype(jnp.bfloat16)
        for c in out_copies(i):
            c.start()

    piece = keep.shape[1]
    group = FEATS // piece

    for f in range(width // FEATS):
        grad = lax.dot_general(
            agg[:, f * FEATS:(f + 1) * FEATS], dbuf[...],
            (((0,), (0,)), ((), ())), preferred_element_type=jnp.float32,
        ).astype(jnp.bfloat16)
        for n in range(group):
            at = f * group + n
            rows = grad[n * piece:(n + 1) * piece]

            @pl.when(core == at % 2)
            def _():
                keep[at // 2] = rows

            @pl.when(core != at % 2)
            def _():
                send[at // 2] = rows

    @pl.loop(0, steps)
    def _(i):
        for c in out_copies(i):
            c.wait()


def call_update(src, count, far, blocks, acc, weight, z_old, dual, target, rho, beta, piece):
    comms, slots, nodes, _ = far.shape
    width, hidden = weight.shape
    flat = comms * nodes
    steps = flat // ROWS
    wide = jax.ShapeDtypeStruct((flat, hidden), jnp.bfloat16)
    half = jax.ShapeDtypeStruct((width // piece // 2, piece, hidden), jnp.bfloat16)
    return pl.pallas_call(
        update,
        out_shape=(wide, wide, half, half),
        in_specs=[SMEM, SMEM] + [VMEM] * 11,
        out_specs=(HBM, HBM, VMEM, VMEM),
        scratch_shapes=[
            pltpu.VMEM((flat, width), jnp.bfloat16),
            pltpu.VMEM((ROWS, width), jnp.float32),
            pltpu.VMEM((flat, hidden), jnp.bfloat16),
            pltpu.VMEM((flat, hidden), jnp.bfloat16),
            pltpu.SemaphoreType.DMA((2, steps)),
        ],
        compiler_params=pltpu.CompilerParams(vmem_limit_bytes=18 * 2**20),
        cost_estimate=pl.CostEstimate(
            flops=4 * flat * width * hidden + 3 * 2 * nodes * nodes * width,
            bytes_accessed=6 * 2**20,
            transcendentals=0,
        ),
        name="update",
    )(src, count, far, *blocks, acc, weight, z_old, dual, target, rho[None], beta[None])


def arrange(first, *refs):
    out = refs[-1]
    for d, part in enumerate(refs[:-1]):
        out[lax.rem(first() + d, len(refs) - 1)] = part[...]


def call_arrange(first, parts, name):
    shape = jax.ShapeDtypeStruct((len(parts), *parts[0].shape), parts[0].dtype)
    return pl.pallas_call(
        functools.partial(arrange, first),
        out_shape=shape,
        in_specs=[VMEM] * len(parts),
        out_specs=VMEM,
        compiler_params=pltpu.CompilerParams(vmem_limit_bytes=2**20),
        cost_estimate=SMALL,
        name=name,
    )(*parts)


def my_y():
    return lax.axis_index("wide") // 8


def my_z():
    return lax.rem(lax.axis_index("wide") // 2, 4)


def my_core():
    return lax.rem(lax.axis_index("wide"), 2)


def pair(mine, other, out):
    core = my_core()

    @pl.loop(0, mine.shape[0])
    def _(i):
        out[i, core] = mine[i]
        out[i, 1 - core] = other[i]


def call_pair(mine, other):
    groups, piece, hidden = mine.shape
    return pl.pallas_call(
        pair,
        out_shape=jax.ShapeDtypeStruct((groups, 2, piece, hidden), mine.dtype),
        in_specs=[VMEM, VMEM],
        out_specs=VMEM,
        compiler_params=pltpu.CompilerParams(vmem_limit_bytes=2**20),
        cost_estimate=SMALL,
        name="pair_rows",
    )(mine, other)


def weight_of_z(rows):
    return call_arrange(my_z, [rows] + [along_z(rows, 4 - d) for d in (1, 2, 3)], "rows_of_z")


def whole_weight(parts):
    piece, hidden = parts.shape[1:]
    parts = call_arrange(my_y, [parts] + [along_y(parts, 4 - d) for d in (1, 2, 3)], "rows_of_y")
    parts = parts.reshape(16, piece, hidden)
    return call_pair(parts, along_core(parts)).reshape(32 * piece, hidden)


def reduced(keep, send, factor):
    y, z, _ = place(lax.axis_index("wide"))
    pick = functools.partial(lax.dynamic_index_in_dim, keepdims=False)
    f32 = lambda x: x.astype(jnp.float32)
    parts = (f32(keep) + f32(along_core(send))).astype(jnp.bfloat16)
    parts = parts.reshape(4, 4, *keep.shape[1:])
    held = f32(pick(parts, z, 1))
    for step in (1, 2, 3):
        held = held + f32(along_z(pick(parts, (z + step) % 4, 1), step))
    parts = held.astype(jnp.bfloat16)
    held = f32(pick(parts, y, 0))
    for step in (1, 2, 3):
        held = held + f32(along_y(pick(parts, (y + step) % 4, 0), step))
    mine = held.astype(jnp.bfloat16)
    held = f32(mine)
    for step in (1, 2, 3):
        held = held + f32(along_comm(mine, step))
    return held * factor


def local(feats, tiles, tile_src, tile_count, request, z_old, dual, target, w_rows, rho, beta):
    comms, nodes, width = feats.shape
    piece, hidden = w_rows.shape
    asks = [along_comm(request, rel) for rel in (1, 2, 3)]
    of_z, *asks = lax.optimization_barrier((weight_of_z(w_rows), *asks))
    chosen = call_choose(asks, feats)
    tiles, of_z, *chosen = lax.optimization_barrier((tiles, of_z, *chosen))
    heads = [along_comm(chosen[2 * n], 3 - n) for n in range(3)]
    near, far_off = [heads[0], heads[2]], [heads[1]]
    last1, last3, *near = lax.optimization_barrier((chosen[1], chosen[5], *near))
    last2, *far_off = lax.optimization_barrier((chosen[3], *far_off))
    heads = near[0], far_off[0], near[1]
    blocks = [along_comm(block, 3 - n) for n, block in enumerate((last1, last2, last3))]
    flat = lambda x: x.reshape(comms * nodes, hidden)
    acc, far, zs, ds, ts = call_own_products(
        tile_src, tile_count, request, feats, tiles, flat(z_old), flat(dual), flat(target)
    )
    weight = whole_weight(of_z)
    acc = call_head_products(tile_src, tile_count, far, heads, acc)
    new_z, new_dual, keep, send = call_update(
        tile_src, tile_count, far, blocks, acc, weight, zs, ds, ts, rho, beta, piece
    )
    total_nodes = comms * nodes * lax.axis_size("comm") * lax.axis_size("wide")
    grad = reduced(keep, send, 1.0 / math.sqrt(total_nodes))
    return new_z.reshape(z_old.shape), new_dual.reshape(z_old.shape), grad


def solution(mesh):
    split = P(("comm", "wide"))
    in_specs = (split,) * 8 + (P("wide"), P(), P())
    out_specs = (split, split, P("wide"))
    return jax.shard_map(local, mesh=mesh, in_specs=in_specs, out_specs=out_specs, check_vma=False)
```

time: 156 us -> 124 us (0.79); the launches traced: 156 us -> 126 us
  local copies, waits for them, and re-layouts: 24.3 us -> 1.35 us
  between operations: 20 us -> 0.91 us
  starting transfers between devices: 23.1 us -> 41.1 us
  waiting for transfers between devices: 67.7 us -> 58.3 us
  Pallas kernels: 14.9 us -> 23.3 us
  matrix products: 4.59 us -> 0 us
    ppermute x16 -> x26, starting transfers between devices: 23 us -> 41.1 us  [shifted(): return lax.ppermute(x, axis, [(i, to(i)) for i in range(size)])]
    unnamed x28 -> x14, local copies, waits for them, and re-layouts: 18.3 us -> 1.28 us
    ppermute x16 -> x26, waiting for transfers between devices: 67 us -> 58.3 us  [shifted(): return lax.ppermute(x, axis, [(i, to(i)) for i in range(size)])]
    pallas_call x2 -> x7, Pallas kernels: 14.9 us -> 23.3 us  [the longest x1 11.6 us: call_update(): pl.pallas_call(update, out_shape=(wide, wide, half, half), in_specs=[SMEM...]
    dot_general x1 -> x0, matrix products: 4.59 us -> none  [local(): jnp.einsum('nf,nh->fh', agg, new_dual, preferred_element_type=jnp.float32)]
    squeeze x1 -> x0, local copies, waits for them, and re-layouts: 4.03 us -> none  [local(): block = lax.dynamic_index_in_dim(feats, asked, 0, keepdims=False)]
    dynamic_slice x5 -> x0, local copies, waits for them, and re-layouts: 1.94 us -> none  [the longest x3 1.75 us: local(): asked = along_comm(request, rel)[0, me]]
  transfers between devices with their start and end apart: 17 -> 26, of which waited for: 13 -> 18; matrix products, arithmetic and copies ran while one was open for 4% -> 0% of each run, Pallas kernels for 3% -> 7%
where the time goes in v2:
time: 124 us; the launch traced here: 126 us
  waiting for transfers between devices  58.3 us (47%)
  starting transfers between devices  41.1 us (33%)
  Pallas kernels  23.3 us (19%)
  local copies, waits for them, and re-layouts  1.35 us (1%)
    ppermute x26, waiting for transfers between devices, shifted(): return lax.ppermute(x, axis, [(i, to(i)) for i in range(size)])  58.3 us
    ppermute x26, starting transfers between devices, shifted(): return lax.ppermute(x, axis, [(i, to(i)) for i in range(size)])  41.1 us
    pallas_call x1, Pallas kernels, call_update(): pl.pallas_call(update, out_shape=(wide, wide, half, half), in_specs=[SMEM...  11.6 us
    pallas_call x1, Pallas kernels, call_own_products(): pl.pallas_call(own_products, out_shape=(jax.ShapeDtypeStruct((comms, node...  6.04 us
    pallas_call x1, Pallas kernels, call_head_products(): pl.pallas_call(head_products, out_shape=jax.ShapeDtypeStruct(acc.shape, a...  2.81 us
    pallas_call x1, Pallas kernels, call_choose(): pl.pallas_call(choose, out_shape=shapes, in_specs=[SMEM] * 3 + [HBM], out...  2.57 us
  transfers between devices with their start and end apart: 26, of which 18 were waited for; matrix products, arithmetic and copies ran while one was open for 0% of the time, Pallas kernels for 7%

profile of v2, /device:TPU:0, one launch (start us, length us, event | category | flops | bytes accessed | tf_op | source)
XLA Modules:
  0.0 126.1 jit_solution(4172720711177318145)
XLA Ops:
  0.6 4.2 %collective-permute-start = (bf16[24,1024]{1,0:T(8,128)(2,1)}, bf16[24,1024]{1,0:T(8,128)(2,1)S(1)}, u32[]{:S(2)}, u32[]{:S(2)}) collective-permute-start(bf16[24,1024]{1,0:T(8,128)(2,1)} %refs_0_.1), channel_id=1, source_target_pairs={{0,6},{1,7},{2,0},{3,1},{4,2},{5,3},{6,4},{7,5},{8,14},{9,15},{10,... | collective-permute-start | bytes 147464 | tf_op jit(solution)/shard_map/ppermute | solution.py:23
  7.6 2.7 %collective-permute-start.4 = (s32[1,4]{1,0:T(1,128)}, s32[1,4]{1,0:T(1,128)S(1)}, u32[]{:S(2)}, u32[]{:S(2)}) collective-permute-start(s32[1,4]{1,0:T(1,128)} %request.1), channel_id=1, source_target_pairs={{0,64},{32,96},{64,0},{96,32},{1,65},{33,97},{65,1},{97,33},{2,66}... | collective-permute-start | bytes 56 | tf_op jit(solution)/shard_map/ppermute | solution.py:23
  14.0 2.6 %choose.1 = (bf16[768,512]{1,0:T(8,128)(2,1)S(1)}, bf16[768,256]{1,0:T(8,128)(2,1)S(1)}, bf16[768,256]{1,0:T(8,128)(2,1)S(1)}, bf16[768,512]{1,0:T(8,128)(2,1)S(...) custom-call(s32[1,4]{1,0:T(1,128)S(1)} %collective-permute-done.3.ask1, ...), custom_call_target="tpu_custom_call" | custom-call | flops 1048576 | bytes 65536 | tf_op jit(solution)/shard_map/choose/pallas_call | solution.py:79
  16.6 3.2 %collective-permute-start.12 = (bf16[4,24,1024]{2,1,0:T(8,128)(2,1)S(1)}, bf16[4,24,1024]{2,1,0:T(8,128)(2,1)S(1)}, u32[]{:S(2)}, u32[]{:S(2)}) collective-permute-start(bf16[4,24,1024]{2,1,0:T(8,128)(2,1)S(1)} %rows_of_z.1.refs_0_), channel_id=1, source_target_pairs={{0,24},{1,25},{2,26},{3,27},{4,28},{5,29},{6,30},{7,31},{8,0},{9,1... | collective-permute-start | bytes 589832 | tf_op jit(solution)/shard_map/ppermute | solution.py:23
  19.8 2.5 %collective-permute-start.6 = (bf16[768,512]{1,0:T(8,128)(2,1)S(1)}, bf16[768,512]{1,0:T(8,128)(2,1)S(1)}, u32[]{:S(2)}, u32[]{:S(2)}) collective-permute-start(bf16[768,512]{1,0:T(8,128)(2,1)S(1)} %get-tuple-element.50), channel_id=1, source_target_pairs={{0,96},{32,0},{64,32},{96,64},{1,97},{33,1},{65,33},{97,65},{2,98}... | collective-permute-start | bytes 2359304 | tf_op jit(solution)/shard_map/ppermute | solution.py:23
  25.7 5.3 %collective-permute-done.13.refs_2_ = bf16[4,24,1024]{2,1,0:T(8,128)(2,1)S(1)} collective-permute-done((bf16[4,24,1024]{2,1,0:T(8,128)(2,1)S(1)}, bf16[4,24,1024]{2,1,0:T(8,128)(2,1)S(1)}, u32[]{:S(2)}, u32[]{:S(2)}) %collective-permute-start.13) | collective-permute-done | bytes 196640 | tf_op jit(solution)/shard_map/ppermute | solution.py:23
  31.0 2.0 %collective-permute-done.14.refs_3_ = bf16[4,24,1024]{2,1,0:T(8,128)(2,1)S(1)} collective-permute-done((bf16[4,24,1024]{2,1,0:T(8,128)(2,1)S(1)}, bf16[4,24,1024]{2,1,0:T(8,128)(2,1)S(1)}, u32[]{:S(2)}, u32[]{:S(2)}) %collective-permute-start.14) | collective-permute-done | bytes 196640 | tf_op jit(solution)/shard_map/ppermute | solution.py:23
  33.2 13.5 %collective-permute-done.9.head2 = bf16[768,256]{1,0:T(8,128)(2,1)S(1)} collective-permute-done((bf16[768,256]{1,0:T(8,128)(2,1)S(1)}, bf16[768,256]{1,0:T(8,128)(2,1)S(1)}, u32[]{:S(2)}, u32[]{:S(2)}) %collective-permute-start.9) | collective-permute-done | bytes 393248 | tf_op jit(solution)/shard_map/ppermute | solution.py:23
  48.7 10.3 %collective-permute-done.6.head1 = bf16[768,512]{1,0:T(8,128)(2,1)S(1)} collective-permute-done((bf16[768,512]{1,0:T(8,128)(2,1)S(1)}, bf16[768,512]{1,0:T(8,128)(2,1)S(1)}, u32[]{:S(2)}, u32[]{:S(2)}) %collective-permute-start.6) | collective-permute-done | bytes 786464 | tf_op jit(solution)/shard_map/ppermute | solution.py:23
  59.0 4.6 %collective-permute-done.7.head3 = bf16[768,512]{1,0:T(8,128)(2,1)S(1)} collective-permute-done((bf16[768,512]{1,0:T(8,128)(2,1)S(1)}, bf16[768,512]{1,0:T(8,128)(2,1)S(1)}, u32[]{:S(2)}, u32[]{:S(2)}) %collective-permute-start.7) | collective-permute-done | bytes 786464 | tf_op jit(solution)/shard_map/ppermute | solution.py:23
  63.6 2.0 %collective-permute-start.11 = (bf16[768,256]{1,0:T(8,128)(2,1)S(1)}, bf16[768,256]{1,0:T(8,128)(2,1)S(1)}, u32[]{:S(2)}, u32[]{:S(2)}) collective-permute-start(bf16[768,256]{1,0:T(8,128)(2,1)S(1)} %get-tuple-element.56), channel_id=1, source_target_pairs={{0,32},{32,64},{64,96},{96,0},{1,33},{33,65},{65,97},{97,1},{2,34}... | collective-permute-start | bytes 1179656 | tf_op jit(solution)/shard_map/ppermute | solution.py:23
  65.6 6.0 %own_products.1 = (f32[2,768,768]{2,1,0:T(8,128)S(1)}, bf16[2,3,768,768]{3,2,1,0:T(8,128)(2,1)S(1)}, bf16[1536,1024]{1,0:T(8,128)(2,1)S(1)}, bf16[1536,1024]{1,0:T(8,128)(2,1)S(1)}, bf16[1536,1024]{1,0:T(8,128)(2,1)S(1)}) custom-call(s32[2,3]{1,0:T(2,128)S(1)} %copy-done.2, s32[2]{0:T(128)S(1)} %copy-done.3, s32[1,4]{1,0:T(1,128)S(1)} %copy-done.4, ...), custom_call_target="tpu_custom_call" | custom-call | flops 1048576 | bytes 65536 | tf_op jit(solution)/shard_map/own_products/pallas_call | solution.py:152
  71.7 2.8 %head_products.1.acc = f32[2,768,768]{2,1,0:T(8,128)S(1)} custom-call(s32[2,3]{1,0:T(2,128)S(1)} %copy-done.2, s32[2]{0:T(128)S(1)} %copy-done.3, bf16[2,3,768,768]{3,2,1,0:T(8,128)(2,1)S(1)} %get-tuple-element.47.far, bf16[768,512]{1,0:T(8,128)(2,1)S(1)} %collective-permute-done.6.head1, ...), custom_call_target="tpu_custom_call", output_to_operand_aliasing={{}: (6, {})} | custom-call | flops 1048576 | bytes 65536 | tf_op jit(solution)/shard_map/head_products/pallas_call | solution.py:195
  75.2 11.6 %update.1 = (bf16[1536,1024]{1,0:T(8,128)(2,1)}, bf16[1536,1024]{1,0:T(8,128)(2,1)}, bf16[16,24,1024]{2,1,0:T(8,128)(2,1)S(1)}, bf16[16,24,1024]{2,1,0:T(8,128)(2,1)S(1)}) custom-call(s32[2,3]{1,0:T(2,128)S(1)} %copy-done.2, s32[2]{0:T(128)S(1)} %copy-done.3, bf16[2,3,768,768]{3,2,1,0:T(8,128)(2,1)S(1)} %get-tuple-element.47.far, ...), custom_call_target="tpu_custom_call" | custom-call | flops 7549747200 | bytes 6291456 | tf_op jit(solution)/shard_map/update/pallas_call | solution.py:291
  87.0 2.2 %collective-permute-done.16 = bf16[16,24,1024]{2,1,0:T(8,128)(2,1)S(1)} collective-permute-done((bf16[16,24,1024]{2,1,0:T(8,128)(2,1)S(1)}, bf16[16,24,1024]{2,1,0:T(8,128)(2,1)S(1)}, u32[]{:S(2)}, u32[]{:S(2)}) %collective-permute-start.16) | collective-permute-done | bytes 786464 | tf_op jit(solution)/shard_map/ppermute | solution.py:23
  90.3 4.2 %collective-permute-start.18 = (bf16[4,24,1024]{2,1,0:T(8,128)(2,1)S(1)}, bf16[4,24,1024]{2,1,0:T(8,128)(2,1)S(1)}, u32[]{:S(2)}, u32[]{:S(2)}) collective-permute-start(bf16[4,24,1024]{2,1,0:T(8,128)(2,1)S(1)} %get-tuple-element.71), channel_id=1, source_target_pairs={{0,4},{1,5},{2,6},{3,7},{4,0},{5,1},{6,2},{7,3},{8,12},{9,13},{10,... | collective-permute-start | bytes 589832 | tf_op jit(solution)/shard_map/ppermute | solution.py:23
  95.6 2.5 %collective-permute-done.19 = bf16[4,24,1024]{2,1,0:T(8,128)(2,1)S(1)} collective-permute-done((bf16[4,24,1024]{2,1,0:T(8,128)(2,1)S(1)}, bf16[4,24,1024]{2,1,0:T(8,128)(2,1)S(1)}, u32[]{:S(2)}, u32[]{:S(2)}) %collective-permute-start.19) | collective-permute-done | bytes 196640 | tf_op jit(solution)/shard_map/ppermute | solution.py:23
  98.0 2.1 %collective-permute-done.18 = bf16[4,24,1024]{2,1,0:T(8,128)(2,1)S(1)} collective-permute-done((bf16[4,24,1024]{2,1,0:T(8,128)(2,1)S(1)}, bf16[4,24,1024]{2,1,0:T(8,128)(2,1)S(1)}, u32[]{:S(2)}, u32[]{:S(2)}) %collective-permute-start.18) | collective-permute-done | bytes 196640 | tf_op jit(solution)/shard_map/ppermute | solution.py:23
  100.1 3.5 %collective-permute-done.17 = bf16[4,24,1024]{2,1,0:T(8,128)(2,1)S(1)} collective-permute-done((bf16[4,24,1024]{2,1,0:T(8,128)(2,1)S(1)}, bf16[4,24,1024]{2,1,0:T(8,128)(2,1)S(1)}, u32[]{:S(2)}, u32[]{:S(2)}) %collective-permute-start.17) | collective-permute-done | bytes 196640 | tf_op jit(solution)/shard_map/ppermute | solution.py:23
  103.8 3.9 %collective-permute-start.22 = (bf16[24,1024]{1,0:T(8,128)(2,1)S(1)}, bf16[24,1024]{1,0:T(8,128)(2,1)S(1)}, u32[]{:S(2)}, u32[]{:S(2)}) collective-permute-start(bf16[24,1024]{1,0:T(8,128)(2,1)S(1)} %get-tuple-element.73), channel_id=1, source_target_pairs={{0,24},{1,25},{2,26},{3,27},{4,28},{5,29},{6,30},{7,31},{8,0},{9,1... | collective-permute-start | bytes 147464 | tf_op jit(solution)/shard_map/ppermute | solution.py:23
  107.7 3.8 %collective-permute-start.21 = (bf16[24,1024]{1,0:T(8,128)(2,1)S(1)}, bf16[24,1024]{1,0:T(8,128)(2,1)S(1)}, u32[]{:S(2)}, u32[]{:S(2)}) collective-permute-start(bf16[24,1024]{1,0:T(8,128)(2,1)S(1)} %get-tuple-element.74), channel_id=1, source_target_pairs={{0,16},{1,17},{2,18},{3,19},{4,20},{5,21},{6,22},{7,23},{8,24},{9,... | collective-permute-start | bytes 147464 | tf_op jit(solution)/shard_map/ppermute | solution.py:23
  113.5 3.2 %collective-permute-done.20 = bf16[24,1024]{1,0:T(8,128)(2,1)S(1)} collective-permute-done((bf16[24,1024]{1,0:T(8,128)(2,1)S(1)}, bf16[24,1024]{1,0:T(8,128)(2,1)S(1)}, u32[]{:S(2)}, u32[]{:S(2)}) %collective-permute-start.20) | collective-permute-done | bytes 49184 | tf_op jit(solution)/shard_map/ppermute | solution.py:23
  116.8 2.8 %collective-permute-start.25 = (bf16[24,1024]{1,0:T(8,128)(2,1)S(1)}, bf16[24,1024]{1,0:T(8,128)(2,1)S(1)}, u32[]{:S(2)}, u32[]{:S(2)}) collective-permute-start(bf16[24,1024]{1,0:T(8,128)(2,1)S(1)} %fusion.5), channel_id=1, source_target_pairs={{0,96},{32,0},{64,32},{96,64},{1,97},{33,1},{65,33},{97,65},{2,98}... | collective-permute-start | bytes 147464 | tf_op jit(solution)/shard_map/ppermute | solution.py:23
  121.3 3.9 %collective-permute-done.24 = bf16[24,1024]{1,0:T(8,128)(2,1)S(1)} collective-permute-done((bf16[24,1024]{1,0:T(8,128)(2,1)S(1)}, bf16[24,1024]{1,0:T(8,128)(2,1)S(1)}, u32[]{:S(2)}, u32[]{:S(2)}) %collective-permute-start.24) | collective-permute-done | bytes 49184 | tf_op jit(solution)/shard_map/ppermute | solution.py:23
  (55 shorter events, 19.6 us)
Async XLA Ops:
  0.6 9.7 %collective-permute-start = (bf16[24,1024]{1,0:T(8,128)(2,1)}, bf16[24,1024]{1,0:T(8,128)(2,1)S(1)}, u32[]{:S(2)}, u32[]{:S(2)}) collective-permute-start(bf16[24,1024]{1,0:T(8,128)(2,1)} %refs_0_.1), channel_id=1, source_target_pairs={{0,6},{1,7},{2,0},{3,1},{4,2},{5,3},{6,4},{7,5},{8,14},{9,15},{10,... | collective-permute-start | bytes 147464 | tf_op jit(solution)/shard_map/ppermute | solution.py:23
  4.8 6.9 %collective-permute-start.1 = (bf16[24,1024]{1,0:T(8,128)(2,1)}, bf16[24,1024]{1,0:T(8,128)(2,1)S(1)}, u32[]{:S(2)}, u32[]{:S(2)}) collective-permute-start(bf16[24,1024]{1,0:T(8,128)(2,1)} %refs_0_.1), channel_id=1, source_target_pairs={{0,4},{1,5},{2,6},{3,7},{4,0},{5,1},{6,2},{7,3},{8,12},{9,13},{10,... | collective-permute-start | bytes 147464 | tf_op jit(solution)/shard_map/ppermute | solution.py:23
  4.8 6.9 %collective-permute-start.2 = (bf16[24,1024]{1,0:T(8,128)(2,1)}, bf16[24,1024]{1,0:T(8,128)(2,1)S(1)}, u32[]{:S(2)}, u32[]{:S(2)}) collective-permute-start(bf16[24,1024]{1,0:T(8,128)(2,1)} %refs_0_.1), channel_id=1, source_target_pairs={{0,2},{1,3},{2,4},{3,5},{4,6},{5,7},{6,0},{7,1},{8,10},{9,11},{10,... | collective-permute-start | bytes 147464 | tf_op jit(solution)/shard_map/ppermute | solution.py:23
  6.1 6.5 %collective-permute-start.3 = (s32[1,4]{1,0:T(1,128)}, s32[1,4]{1,0:T(1,128)S(1)}, u32[]{:S(2)}, u32[]{:S(2)}) collective-permute-start(s32[1,4]{1,0:T(1,128)} %request.1), channel_id=1, source_target_pairs={{0,32},{32,64},{64,96},{96,0},{1,33},{33,65},{65,97},{97,1},{2,34}... | collective-permute-start | bytes 56 | tf_op jit(solution)/shard_map/ppermute | solution.py:23
  7.6 5.2 %collective-permute-start.4 = (s32[1,4]{1,0:T(1,128)}, s32[1,4]{1,0:T(1,128)S(1)}, u32[]{:S(2)}, u32[]{:S(2)}) collective-permute-start(s32[1,4]{1,0:T(1,128)} %request.1), channel_id=1, source_target_pairs={{0,64},{32,96},{64,0},{96,32},{1,65},{33,97},{65,1},{97,33},{2,66}... | collective-permute-start | bytes 56 | tf_op jit(solution)/shard_map/ppermute | solution.py:23
  16.6 8.5 %collective-permute-start.12 = (bf16[4,24,1024]{2,1,0:T(8,128)(2,1)S(1)}, bf16[4,24,1024]{2,1,0:T(8,128)(2,1)S(1)}, u32[]{:S(2)}, u32[]{:S(2)}) collective-permute-start(bf16[4,24,1024]{2,1,0:T(8,128)(2,1)S(1)} %rows_of_z.1.refs_0_), channel_id=1, source_target_pairs={{0,24},{1,25},{2,26},{3,27},{4,28},{5,29},{6,30},{7,31},{8,0},{9,1... | collective-permute-start | bytes 589832 | tf_op jit(solution)/shard_map/ppermute | solution.py:23
  19.8 39.2 %collective-permute-start.6 = (bf16[768,512]{1,0:T(8,128)(2,1)S(1)}, bf16[768,512]{1,0:T(8,128)(2,1)S(1)}, u32[]{:S(2)}, u32[]{:S(2)}) collective-permute-start(bf16[768,512]{1,0:T(8,128)(2,1)S(1)} %get-tuple-element.50), channel_id=1, source_target_pairs={{0,96},{32,0},{64,32},{96,64},{1,97},{33,1},{65,33},{97,65},{2,98}... | collective-permute-start | bytes 2359304 | tf_op jit(solution)/shard_map/ppermute | solution.py:23
  22.3 41.3 %collective-permute-start.7 = (bf16[768,512]{1,0:T(8,128)(2,1)S(1)}, bf16[768,512]{1,0:T(8,128)(2,1)S(1)}, u32[]{:S(2)}, u32[]{:S(2)}) collective-permute-start(bf16[768,512]{1,0:T(8,128)(2,1)S(1)} %get-tuple-element.51), channel_id=1, source_target_pairs={{0,32},{32,64},{64,96},{96,0},{1,33},{33,65},{65,97},{97,1},{2,34}... | collective-permute-start | bytes 2359304 | tf_op jit(solution)/shard_map/ppermute | solution.py:23
  22.3 24.4 %collective-permute-start.9 = (bf16[768,256]{1,0:T(8,128)(2,1)S(1)}, bf16[768,256]{1,0:T(8,128)(2,1)S(1)}, u32[]{:S(2)}, u32[]{:S(2)}) collective-permute-start(bf16[768,256]{1,0:T(8,128)(2,1)S(1)} %get-tuple-element.54), channel_id=1, source_target_pairs={{0,64},{32,96},{64,0},{96,32},{1,65},{33,97},{65,1},{97,33},{2,66}... | collective-permute-start | bytes 1179656 | tf_op jit(solution)/shard_map/ppermute | solution.py:23
  23.8 7.2 %collective-permute-start.13 = (bf16[4,24,1024]{2,1,0:T(8,128)(2,1)S(1)}, bf16[4,24,1024]{2,1,0:T(8,128)(2,1)S(1)}, u32[]{:S(2)}, u32[]{:S(2)}) collective-permute-start(bf16[4,24,1024]{2,1,0:T(8,128)(2,1)S(1)} %rows_of_z.1.refs_0_), channel_id=1, source_target_pairs={{0,16},{1,17},{2,18},{3,19},{4,20},{5,21},{6,22},{7,23},{8,24},{9,... | collective-permute-start | bytes 589832 | tf_op jit(solution)/shard_map/ppermute | solution.py:23
  25.1 7.9 %collective-permute-start.14 = (bf16[4,24,1024]{2,1,0:T(8,128)(2,1)S(1)}, bf16[4,24,1024]{2,1,0:T(8,128)(2,1)S(1)}, u32[]{:S(2)}, u32[]{:S(2)}) collective-permute-start(bf16[4,24,1024]{2,1,0:T(8,128)(2,1)S(1)} %rows_of_z.1.refs_0_), channel_id=1, source_target_pairs={{0,8},{1,9},{2,10},{3,11},{4,12},{5,13},{6,14},{7,15},{8,16},{9,17... | collective-permute-start | bytes 589832 | tf_op jit(solution)/shard_map/ppermute | solution.py:23
  33.1 41.4 %collective-permute-start.15 = (bf16[16,24,1024]{2,1,0:T(8,128)(2,1)S(1)}, bf16[16,24,1024]{2,1,0:T(8,128)(2,1)S(1)}, u32[]{:S(2)}, u32[]{:S(2)}) collective-permute-start(bf16[16,24,1024]{2,1,0:T(8,128)(2,1)S(1)} %bitcast.30), channel_id=1, source_target_pairs={{0,1},{1,0},{2,3},{3,2},{4,5},{5,4},{6,7},{7,6},{8,9},{9,8},{10,11... | collective-permute-start | bytes 2359304 | tf_op jit(solution)/shard_map/ppermute | solution.py:23
  46.7 28.0 %collective-permute-start.10 = (bf16[768,512]{1,0:T(8,128)(2,1)S(1)}, bf16[768,512]{1,0:T(8,128)(2,1)S(1)}, u32[]{:S(2)}, u32[]{:S(2)}) collective-permute-start(bf16[768,512]{1,0:T(8,128)(2,1)S(1)} %get-tuple-element.55), channel_id=1, source_target_pairs={{0,64},{32,96},{64,0},{96,32},{1,65},{33,97},{65,1},{97,33},{2,66}... | collective-permute-start | bytes 2359304 | tf_op jit(solution)/shard_map/ppermute | solution.py:23
  63.6 11.1 %collective-permute-start.8 = (bf16[768,256]{1,0:T(8,128)(2,1)S(1)}, bf16[768,256]{1,0:T(8,128)(2,1)S(1)}, u32[]{:S(2)}, u32[]{:S(2)}) collective-permute-start(bf16[768,256]{1,0:T(8,128)(2,1)S(1)} %get-tuple-element.52), channel_id=1, source_target_pairs={{0,96},{32,0},{64,32},{96,64},{1,97},{33,1},{65,33},{97,65},{2,98}... | collective-permute-start | bytes 1179656 | tf_op jit(solution)/shard_map/ppermute | solution.py:23
  63.6 11.1 %collective-permute-start.11 = (bf16[768,256]{1,0:T(8,128)(2,1)S(1)}, bf16[768,256]{1,0:T(8,128)(2,1)S(1)}, u32[]{:S(2)}, u32[]{:S(2)}) collective-permute-start(bf16[768,256]{1,0:T(8,128)(2,1)S(1)} %get-tuple-element.56), channel_id=1, source_target_pairs={{0,32},{32,64},{64,96},{96,0},{1,33},{33,65},{65,97},{97,1},{2,34}... | collective-permute-start | bytes 1179656 | tf_op jit(solution)/shard_map/ppermute | solution.py:23
  89.5 8.5 %collective-permute-start.19 = (bf16[4,24,1024]{2,1,0:T(8,128)(2,1)S(1)}, bf16[4,24,1024]{2,1,0:T(8,128)(2,1)S(1)}, u32[]{:S(2)}, u32[]{:S(2)}) collective-permute-start(bf16[4,24,1024]{2,1,0:T(8,128)(2,1)S(1)} %get-tuple-element.70), channel_id=1, source_target_pairs={{0,6},{1,7},{2,0},{3,1},{4,2},{5,3},{6,4},{7,5},{8,14},{9,15},{10,... | collective-permute-start | bytes 589832 | tf_op jit(solution)/shard_map/ppermute | solution.py:23
  90.3 9.9 %collective-permute-start.18 = (bf16[4,24,1024]{2,1,0:T(8,128)(2,1)S(1)}, bf16[4,24,1024]{2,1,0:T(8,128)(2,1)S(1)}, u32[]{:S(2)}, u32[]{:S(2)}) collective-permute-start(bf16[4,24,1024]{2,1,0:T(8,128)(2,1)S(1)} %get-tuple-element.71), channel_id=1, source_target_pairs={{0,4},{1,5},{2,6},{3,7},{4,0},{5,1},{6,2},{7,3},{8,12},{9,13},{10,... | collective-permute-start | bytes 589832 | tf_op jit(solution)/shard_map/ppermute | solution.py:23
  94.4 9.2 %collective-permute-start.17 = (bf16[4,24,1024]{2,1,0:T(8,128)(2,1)S(1)}, bf16[4,24,1024]{2,1,0:T(8,128)(2,1)S(1)}, u32[]{:S(2)}, u32[]{:S(2)}) collective-permute-start(bf16[4,24,1024]{2,1,0:T(8,128)(2,1)S(1)} %get-tuple-element.69), channel_id=1, source_target_pairs={{0,2},{1,3},{2,4},{3,5},{4,6},{5,7},{6,0},{7,1},{8,10},{9,11},{10,... | collective-permute-start | bytes 589832 | tf_op jit(solution)/shard_map/ppermute | solution.py:23
  103.8 7.7 %collective-permute-start.22 = (bf16[24,1024]{1,0:T(8,128)(2,1)S(1)}, bf16[24,1024]{1,0:T(8,128)(2,1)S(1)}, u32[]{:S(2)}, u32[]{:S(2)}) collective-permute-start(bf16[24,1024]{1,0:T(8,128)(2,1)S(1)} %get-tuple-element.73), channel_id=1, source_target_pairs={{0,24},{1,25},{2,26},{3,27},{4,28},{5,29},{6,30},{7,31},{8,0},{9,1... | collective-permute-start | bytes 147464 | tf_op jit(solution)/shard_map/ppermute | solution.py:23
  107.7 5.8 %collective-permute-start.21 = (bf16[24,1024]{1,0:T(8,128)(2,1)S(1)}, bf16[24,1024]{1,0:T(8,128)(2,1)S(1)}, u32[]{:S(2)}, u32[]{:S(2)}) collective-permute-start(bf16[24,1024]{1,0:T(8,128)(2,1)S(1)} %get-tuple-element.74), channel_id=1, source_target_pairs={{0,16},{1,17},{2,18},{3,19},{4,20},{5,21},{6,22},{7,23},{8,24},{9,... | collective-permute-start | bytes 147464 | tf_op jit(solution)/shard_map/ppermute | solution.py:23
  111.4 5.3 %collective-permute-start.20 = (bf16[24,1024]{1,0:T(8,128)(2,1)S(1)}, bf16[24,1024]{1,0:T(8,128)(2,1)S(1)}, u32[]{:S(2)}, u32[]{:S(2)}) collective-permute-start(bf16[24,1024]{1,0:T(8,128)(2,1)S(1)} %get-tuple-element.72), channel_id=1, source_target_pairs={{0,8},{1,9},{2,10},{3,11},{4,12},{5,13},{6,14},{7,15},{8,16},{9,17... | collective-permute-start | bytes 147464 | tf_op jit(solution)/shard_map/ppermute | solution.py:23
  116.8 4.6 %collective-permute-start.25 = (bf16[24,1024]{1,0:T(8,128)(2,1)S(1)}, bf16[24,1024]{1,0:T(8,128)(2,1)S(1)}, u32[]{:S(2)}, u32[]{:S(2)}) collective-permute-start(bf16[24,1024]{1,0:T(8,128)(2,1)S(1)} %fusion.5), channel_id=1, source_target_pairs={{0,96},{32,0},{64,32},{96,64},{1,97},{33,1},{65,33},{97,65},{2,98}... | collective-permute-start | bytes 147464 | tf_op jit(solution)/shard_map/ppermute | solution.py:23
  119.6 5.7 %collective-permute-start.24 = (bf16[24,1024]{1,0:T(8,128)(2,1)S(1)}, bf16[24,1024]{1,0:T(8,128)(2,1)S(1)}, u32[]{:S(2)}, u32[]{:S(2)}) collective-permute-start(bf16[24,1024]{1,0:T(8,128)(2,1)S(1)} %fusion.5), channel_id=1, source_target_pairs={{0,64},{32,96},{64,0},{96,32},{1,65},{33,97},{65,1},{97,33},{2,66}... | collective-permute-start | bytes 147464 | tf_op jit(solution)/shard_map/ppermute | solution.py:23
  119.6 5.8 %collective-permute-start.23 = (bf16[24,1024]{1,0:T(8,128)(2,1)S(1)}, bf16[24,1024]{1,0:T(8,128)(2,1)S(1)}, u32[]{:S(2)}, u32[]{:S(2)}) collective-permute-start(bf16[24,1024]{1,0:T(8,128)(2,1)S(1)} %fusion.5), channel_id=1, source_target_pairs={{0,32},{32,64},{64,96},{96,0},{1,33},{33,65},{65,97},{97,1},{2,34}... | collective-permute-start | bytes 147464 | tf_op jit(solution)/shard_map/ppermute | solution.py:23
  (9 other events, 232.4 us)

commit v3 on v2

--- a/solution.py
+++ b/solution.py
@@ -8,10 +8,11 @@
 from jax.experimental.pallas import tpu as pltpu
 from jax.sharding import PartitionSpec as P
 
-ROWS = 256
+ROWS = 768
 COLS = 256
-FEATS = 384
-CUTS = (512, 256, 512)
+FEATS = 768
+EARLY = 128
+CUT = 512
 SMALL = pl.CostEstimate(flops=2**20, bytes_accessed=2**16, transcendentals=0)
 SMEM = pl.BlockSpec(memory_space=pltpu.SMEM)
 VMEM = pl.BlockSpec(memory_space=pltpu.VMEM)
@@ -51,17 +52,19 @@
     return lax.axis_index("comm")
 
 
+def pieces(width):
+    return [(start, CUT, width) for start in (0, EARLY, 0)]
+
+
 def choose(ask1, ask2, ask3, feats, *refs):
     outs, sems = refs[:-1], refs[-1]
     me = me_on_comm()
     copies = []
-    for n, ask in enumerate((ask1, ask2, ask3)):
-        asked, cut = ask[0, me], CUTS[n]
-        for part, cols in enumerate((slice(0, cut), slice(cut, feats.shape[2]))):
+    for ask, bounds in zip((ask1, ask2, ask3), pieces(feats.shape[2])):
+        for low, high in zip(bounds[:-1], bounds[1:]):
+            n = len(copies)
             copies.append(
-                pltpu.make_async_copy(
-                    feats.at[asked, :, cols], outs[2 * n + part], sems.at[2 * n + part]
-                )
+                pltpu.make_async_copy(feats.at[ask[0, me], :, low:high], outs[n], sems.at[n])
             )
     for c in copies:
         c.start()
@@ -72,9 +75,9 @@
 def call_choose(asks, feats):
     nodes, width = feats.shape[1:]
     shapes = [
-        jax.ShapeDtypeStruct((nodes, cols), feats.dtype)
-        for cut in CUTS
-        for cols in (cut, width - cut)
+        jax.ShapeDtypeStruct((nodes, high - low), feats.dtype)
+        for bounds in pieces(width)
+        for low, high in zip(bounds[:-1], bounds[1:])
     ]
     return pl.pallas_call(
         choose,
@@ -82,7 +85,7 @@
         in_specs=[SMEM] * 3 + [HBM],
         out_specs=[VMEM] * len(shapes),
         scratch_shapes=[pltpu.SemaphoreType.DMA((len(shapes),))],
-        compiler_params=pltpu.CompilerParams(vmem_limit_bytes=2**20),
+        compiler_params=pltpu.CompilerParams(vmem_limit_bytes=4 * 2**20),
         cost_estimate=SMALL,
         name="choose",
     )(*asks, in_hbm(feats))
@@ -163,7 +166,7 @@
             pltpu.SemaphoreType.DMA((comms, slots)),
             pltpu.SemaphoreType.DMA((3,)),
         ],
-        compiler_params=pltpu.CompilerParams(vmem_limit_bytes=10 * 2**20),
+        compiler_params=pltpu.CompilerParams(vmem_limit_bytes=16 * 2**20),
         cost_estimate=SMALL,
         name="own_products",
     )(src, count, request, feats, *map(in_hbm, (tiles, z_old, dual, target)))
@@ -174,34 +177,44 @@
     return (t < count[k]) & (src[k, t] >= local) & (rel > 0), rel
 
 
-def head_products(src, count, far, head1, head2, head3, before, acc):
-    comms, slots, nodes, _ = far.shape
+def head_products(src, count, request, far, early, head1, head2, head3, before, acc):
+    comms, slots, _, _ = far.shape
+    opposite = request[0, lax.rem(me_on_comm() + 2, 4)]
+
+    def add(k, t, low, block):
+        acc[k, :, low:low + block.shape[1]] += jnp.dot(
+            far[k, t], block, preferred_element_type=jnp.float32
+        )
+
     for k in range(comms):
         for t in range(slots):
             live, rel = relation(src, count, k, t, comms)
-            for r, (block, cut) in enumerate(zip((head1, head2, head3), CUTS), 1):
-
-                @pl.when(live & (rel == r))
-                def _():
-                    @pl.loop(0, nodes // ROWS)
-                    def _(i):
-                        rows = pl.ds(pl.multiple_of(i * ROWS, ROWS), ROWS)
-                        acc[k, rows, :cut] += jnp.dot(
-                            far[k, t, rows, :], block[...], preferred_element_type=jnp.float32
-                        )
-
-
-def call_head_products(src, count, far, heads, acc):
+
+            @pl.when(live & (rel == 1))
+            def _():
+                add(k, t, 0, head1[...])
+
+            @pl.when(live & (rel == 2))
+            def _():
+                add(k, t, 0, early[opposite])
+                add(k, t, EARLY, head2[...])
+
+            @pl.when(live & (rel == 3))
+            def _():
+                add(k, t, 0, head3[...])
+
+
+def call_head_products(src, count, request, far, early, heads, acc):
     return pl.pallas_call(
         head_products,
         out_shape=jax.ShapeDtypeStruct(acc.shape, acc.dtype),
-        in_specs=[SMEM, SMEM] + [VMEM] * 5,
+        in_specs=[SMEM] * 3 + [VMEM] * 6,
         out_specs=VMEM,
-        input_output_aliases={6: 0},
-        compiler_params=pltpu.CompilerParams(vmem_limit_bytes=4 * 2**20),
+        input_output_aliases={8: 0},
+        compiler_params=pltpu.CompilerParams(vmem_limit_bytes=8 * 2**20),
         cost_estimate=SMALL,
         name="head_products",
-    )(src, count, far, *heads, acc)
+    )(src, count, request, far, early, *heads, acc)
 
 
 def update(
@@ -229,11 +242,11 @@
         total[...] = acc[k, rows, :]
         for t in range(slots):
             live, rel = relation(src, count, k, t, comms)
-            for r, (block, cut) in enumerate(zip((from1, from2, from3), CUTS), 1):
+            for r, block in enumerate((from1, from2, from3), 1):
 
                 @pl.when(live & (rel == r))
                 def _():
-                    total[:, cut:] += jnp.dot(
+                    total[:, CUT:] += jnp.dot(
                         far[k, t, rows, :], block[...], preferred_element_type=jnp.float32
                     )
 
@@ -300,7 +313,7 @@
             pltpu.VMEM((flat, hidden), jnp.bfloat16),
             pltpu.SemaphoreType.DMA((2, steps)),
         ],
-        compiler_params=pltpu.CompilerParams(vmem_limit_bytes=18 * 2**20),
+        compiler_params=pltpu.CompilerParams(vmem_limit_bytes=24 * 2**20),
         cost_estimate=pl.CostEstimate(
             flops=4 * flat * width * hidden + 3 * 2 * nodes * nodes * width,
             bytes_accessed=6 * 2**20,
@@ -323,7 +336,7 @@
         out_shape=shape,
         in_specs=[VMEM] * len(parts),
         out_specs=VMEM,
-        compiler_params=pltpu.CompilerParams(vmem_limit_bytes=2**20),
+        compiler_params=pltpu.CompilerParams(vmem_limit_bytes=4 * 2**20),
         cost_estimate=SMALL,
         name=name,
     )(*parts)
@@ -357,7 +370,7 @@
         out_shape=jax.ShapeDtypeStruct((groups, 2, piece, hidden), mine.dtype),
         in_specs=[VMEM, VMEM],
         out_specs=VMEM,
-        compiler_params=pltpu.CompilerParams(vmem_limit_bytes=2**20),
+        compiler_params=pltpu.CompilerParams(vmem_limit_bytes=4 * 2**20),
         cost_estimate=SMALL,
         name="pair_rows",
     )(mine, other)
@@ -367,11 +380,12 @@
     return call_arrange(my_z, [rows] + [along_z(rows, 4 - d) for d in (1, 2, 3)], "rows_of_z")
 
 
-def whole_weight(parts):
+def whole_weight(parts, after):
     piece, hidden = parts.shape[1:]
-    parts = call_arrange(my_y, [parts] + [along_y(parts, 4 - d) for d in (1, 2, 3)], "rows_of_y")
-    parts = parts.reshape(16, piece, hidden)
-    return call_pair(parts, along_core(parts)).reshape(32 * piece, hidden)
+    rows = [parts] + [along_y(parts, 4 - d) for d in (1, 2, 3)]
+    after, *rows = lax.optimization_barrier((after, *rows))
+    parts = call_arrange(my_y, rows, "rows_of_y").reshape(16, piece, hidden)
+    return call_pair(parts, along_core(parts)).reshape(32 * piece, hidden), after
 
 
 def reduced(keep, send, factor):
@@ -398,9 +412,12 @@
     comms, nodes, width = feats.shape
     piece, hidden = w_rows.shape
     asks = [along_comm(request, rel) for rel in (1, 2, 3)]
+    first, w_rows, *asks = lax.optimization_barrier((feats[:, :, :EARLY], w_rows, *asks))
+    early = along_comm(first, 2)
     of_z, *asks = lax.optimization_barrier((weight_of_z(w_rows), *asks))
     chosen = call_choose(asks, feats)
     tiles, of_z, *chosen = lax.optimization_barrier((tiles, of_z, *chosen))
+    early, chosen[2] = lax.optimization_barrier((early, chosen[2]))
     heads = [along_comm(chosen[2 * n], 3 - n) for n in range(3)]
     near, far_off = [heads[0], heads[2]], [heads[1]]
     last1, last3, *near = lax.optimization_barrier((chosen[1], chosen[5], *near))
@@ -411,8 +428,8 @@
     acc, far, zs, ds, ts = call_own_products(
         tile_src, tile_count, request, feats, tiles, flat(z_old), flat(dual), flat(target)
     )
-    weight = whole_weight(of_z)
-    acc = call_head_products(tile_src, tile_count, far, heads, acc)
+    weight, acc = whole_weight(of_z, acc)
+    acc = call_head_products(tile_src, tile_count, request, far, early, heads, acc)
     new_z, new_dual, keep, send = call_update(
         tile_src, tile_count, far, blocks, acc, weight, zs, ds, ts, rho, beta, piece
     )

time: 124 us -> 115 us (0.927); the launches traced: 126 us -> 115 us
  waiting for transfers between devices: 58.3 us -> 51.5 us
  starting transfers between devices: 41.1 us -> 36.4 us
  local copies, waits for them, and re-layouts: 1.35 us -> 3.91 us
  Pallas kernels: 23.3 us -> 20.8 us
    ppermute x26 -> x27, waiting for transfers between devices: 58.3 us -> 51.5 us  [shifted(): return lax.ppermute(x, axis, [(i, to(i)) for i in range(size)])]
    ppermute x26 -> x27, starting transfers between devices: 41.1 us -> 36.4 us  [shifted(): return lax.ppermute(x, axis, [(i, to(i)) for i in range(size)])]
    pallas_call x1, Pallas kernels: 11.6 us -> 9.33 us  [call_update(): pl.pallas_call(update, out_shape=(wide, wide, half, half), in_specs=[SMEM...]
    unnamed x14 -> x18, local copies, waits for them, and re-layouts: 1.28 us -> 2.82 us
  transfers between devices with their start and end apart: 26 -> 27, of which waited for: 18 -> 19; matrix products, arithmetic and copies ran while one was open for 0% -> 1% of each run, Pallas kernels for 7% -> 10%
where the time goes in v3:
time: 115 us
  waiting for transfers between devices  51.5 us (45%)
  starting transfers between devices  36.4 us (32%)
  Pallas kernels  20.8 us (18%)
  local copies, waits for them, and re-layouts  3.91 us (3%)
    ppermute x27, waiting for transfers between devices, shifted(): return lax.ppermute(x, axis, [(i, to(i)) for i in range(size)])  51.5 us
    ppermute x27, starting transfers between devices, shifted(): return lax.ppermute(x, axis, [(i, to(i)) for i in range(size)])  36.4 us
    pallas_call x1, Pallas kernels, call_update(): pl.pallas_call(update, out_shape=(wide, wide, half, half), in_specs=[SMEM...  9.33 us
    pallas_call x1, Pallas kernels, call_own_products(): pl.pallas_call(own_products, out_shape=(jax.ShapeDtypeStruct((comms, node...  6.02 us
    unnamed x18, local copies, waits for them, and re-layouts  2.82 us
    pallas_call x1, Pallas kernels, call_head_products(): pl.pallas_call(head_products, out_shape=jax.ShapeDtypeStruct(acc.shape, a...  2.64 us
    pallas_call x1, Pallas kernels, call_choose(): pl.pallas_call(choose, out_shape=shapes, in_specs=[SMEM] * 3 + [HBM], out...  2.51 us
  transfers between devices with their start and end apart: 27, of which 19 were waited for; matrix products, arithmetic and copies ran while one was open for 1% of the time, Pallas kernels for 10%

profile of v3, /device:TPU:0, one launch (start us, length us, event | category | flops | bytes accessed | tf_op | source)
XLA Modules:
  0.0 114.7 jit_solution(6031450802154054654)
XLA Ops:
  0.6 1.6 %collective-permute-start = (s32[1,4]{1,0:T(1,128)}, s32[1,4]{1,0:T(1,128)S(1)}, u32[]{:S(2)}, u32[]{:S(2)}) collective-permute-start(s32[1,4]{1,0:T(1,128)} %request.3), channel_id=1, source_target_pairs={{0,32},{32,64},{64,96},{96,0},{1,33},{33,65},{65,97},{97,1},{2,34}... | collective-permute-start | bytes 56 | tf_op jit(solution)/shard_map/ppermute | solution.py:24
  2.3 2.7 %collective-permute-start.1 = (s32[1,4]{1,0:T(1,128)}, s32[1,4]{1,0:T(1,128)S(1)}, u32[]{:S(2)}, u32[]{:S(2)}) collective-permute-start(s32[1,4]{1,0:T(1,128)} %request.3), channel_id=1, source_target_pairs={{0,64},{32,96},{64,0},{96,32},{1,65},{33,97},{65,1},{97,33},{2,66}... | collective-permute-start | bytes 56 | tf_op jit(solution)/shard_map/ppermute | solution.py:24
  10.2 4.0 %collective-permute-start.3 = (bf16[24,1024]{1,0:T(8,128)(2,1)}, bf16[24,1024]{1,0:T(8,128)(2,1)S(1)}, u32[]{:S(2)}, u32[]{:S(2)}) collective-permute-start(bf16[24,1024]{1,0:T(8,128)(2,1)} %refs_0_), channel_id=1, source_target_pairs={{0,6},{1,7},{2,0},{3,1},{4,2},{5,3},{6,4},{7,5},{8,14},{9,15},{10,... | collective-permute-start | bytes 147464 | tf_op jit(solution)/shard_map/ppermute | solution.py:24
  16.3 3.8 %collective-permute-done.4.refs_2_ = bf16[24,1024]{1,0:T(8,128)(2,1)S(1)} collective-permute-done((bf16[24,1024]{1,0:T(8,128)(2,1)}, bf16[24,1024]{1,0:T(8,128)(2,1)S(1)}, u32[]{:S(2)}, u32[]{:S(2)}) %collective-permute-start.4) | collective-permute-done | bytes 49184 | tf_op jit(solution)/shard_map/ppermute | solution.py:24
  21.1 2.5 %choose.1 = (bf16[768,512]{1,0:T(8,128)(2,1)S(1)}, bf16[768,256]{1,0:T(8,128)(2,1)S(1)}, bf16[768,384]{1,0:T(8,128)(2,1)S(1)}, bf16[768,256]{1,0:T(8,128)(2,1)S(...) custom-call(s32[1,4]{1,0:T(1,128)S(1)} %collective-permute-done.ask1, ...), custom_call_target="tpu_custom_call" | custom-call | flops 1048576 | bytes 65536 | tf_op jit(solution)/shard_map/choose/pallas_call | solution.py:82
  23.6 1.9 %collective-permute-start.6 = (bf16[768,512]{1,0:T(8,128)(2,1)S(1)}, bf16[768,512]{1,0:T(8,128)(2,1)S(1)}, u32[]{:S(2)}, u32[]{:S(2)}) collective-permute-start(bf16[768,512]{1,0:T(8,128)(2,1)S(1)} %get-tuple-element.66), channel_id=1, source_target_pairs={{0,96},{32,0},{64,32},{96,64},{1,97},{33,1},{65,33},{97,65},{2,98}... | collective-permute-start | bytes 2359304 | tf_op jit(solution)/shard_map/ppermute | solution.py:24
  25.8 3.3 %collective-permute-start.13 = (bf16[4,24,1024]{2,1,0:T(8,128)(2,1)S(1)}, bf16[4,24,1024]{2,1,0:T(8,128)(2,1)S(1)}, u32[]{:S(2)}, u32[]{:S(2)}) collective-permute-start(bf16[4,24,1024]{2,1,0:T(8,128)(2,1)S(1)} %rows_of_z.1.refs_0_), channel_id=1, source_target_pairs={{0,24},{1,25},{2,26},{3,27},{4,28},{5,29},{6,30},{7,31},{8,0},{9,1... | collective-permute-start | bytes 589832 | tf_op jit(solution)/shard_map/ppermute | solution.py:24
  30.7 3.7 %collective-permute-done.13.refs_1_ = bf16[4,24,1024]{2,1,0:T(8,128)(2,1)S(1)} collective-permute-done((bf16[4,24,1024]{2,1,0:T(8,128)(2,1)S(1)}, bf16[4,24,1024]{2,1,0:T(8,128)(2,1)S(1)}, u32[]{:S(2)}, u32[]{:S(2)}) %collective-permute-start.13) | collective-permute-done | bytes 196640 | tf_op jit(solution)/shard_map/ppermute | solution.py:24
  34.4 1.7 %collective-permute-start.10 = (bf16[768,384]{1,0:T(8,128)(2,1)S(1)}, bf16[768,384]{1,0:T(8,128)(2,1)S(1)}, u32[]{:S(2)}, u32[]{:S(2)}) collective-permute-start(bf16[768,384]{1,0:T(8,128)(2,1)S(1)} %get-tuple-element.72), channel_id=1, source_target_pairs={{0,64},{32,96},{64,0},{96,32},{1,65},{33,97},{65,1},{97,33},{2,66}... | collective-permute-start | bytes 1769480 | tf_op jit(solution)/shard_map/ppermute | solution.py:24
  38.1 6.0 %own_products.1 = (f32[2,768,768]{2,1,0:T(8,128)S(1)}, bf16[2,3,768,768]{3,2,1,0:T(8,128)(2,1)S(1)}, bf16[1536,1024]{1,0:T(8,128)(2,1)S(1)}, bf16[1536,1024]{1,0:T(8,128)(2,1)S(1)}, bf16[1536,1024]{1,0:T(8,128)(2,1)S(1)}) custom-call(s32[2,3]{1,0:T(2,128)S(1)} %copy-done.2, s32[2]{0:T(128)S(1)} %copy-done.5, s32[1,4]{1,0:T(1,128)S(1)} %copy-done.4, ...), custom_call_target="tpu_custom_call" | custom-call | flops 1048576 | bytes 65536 | tf_op jit(solution)/shard_map/own_products/pallas_call | solution.py:155
  44.4 7.1 %collective-permute-done.7.head3 = bf16[768,512]{1,0:T(8,128)(2,1)S(1)} collective-permute-done((bf16[768,512]{1,0:T(8,128)(2,1)S(1)}, bf16[768,512]{1,0:T(8,128)(2,1)S(1)}, u32[]{:S(2)}, u32[]{:S(2)}) %collective-permute-start.7) | collective-permute-done | bytes 786464 | tf_op jit(solution)/shard_map/ppermute | solution.py:24
  51.5 2.0 %collective-permute-start.12 = (bf16[768,256]{1,0:T(8,128)(2,1)S(1)}, bf16[768,256]{1,0:T(8,128)(2,1)S(1)}, u32[]{:S(2)}, u32[]{:S(2)}) collective-permute-start(bf16[768,256]{1,0:T(8,128)(2,1)S(1)} %get-tuple-element.74), channel_id=1, source_target_pairs={{0,32},{32,64},{64,96},{96,0},{1,33},{33,65},{65,97},{97,1},{2,34}... | collective-permute-start | bytes 1179656 | tf_op jit(solution)/shard_map/ppermute | solution.py:24
  53.5 5.4 %collective-permute-done.10.head2 = bf16[768,384]{1,0:T(8,128)(2,1)S(1)} collective-permute-done((bf16[768,384]{1,0:T(8,128)(2,1)S(1)}, bf16[768,384]{1,0:T(8,128)(2,1)S(1)}, u32[]{:S(2)}, u32[]{:S(2)}) %collective-permute-start.10) | collective-permute-done | bytes 589856 | tf_op jit(solution)/shard_map/ppermute | solution.py:24
  60.0 2.6 %head_products.1.acc = f32[2,768,768]{2,1,0:T(8,128)S(1)} custom-call(s32[2,3]{1,0:T(2,128)S(1)} %copy-done.2, s32[2]{0:T(128)S(1)} %copy-done.5, s32[1,4]{1,0:T(1,128)S(1)} %copy-done.4, bf16[2,3,768,768]{3,2,1,0:T(8,128)(2,1)S(1)} %get-tuple-element.63.far, bf16[2,768,128]{2,1,0:T(8,128)(2,1)S(1)} %collective-permute-done.9.early, ...), custom_call_target="tpu_custom_call", output_to_operand_aliasing={{}: (8, {})} | custom-call | flops 1048576 | bytes 65536 | tf_op jit(solution)/shard_map/head_products/pallas_call | solution.py:208
  62.9 2.3 %collective-permute-done.8.from1 = bf16[768,256]{1,0:T(8,128)(2,1)S(1)} collective-permute-done((bf16[768,256]{1,0:T(8,128)(2,1)S(1)}, bf16[768,256]{1,0:T(8,128)(2,1)S(1)}, u32[]{:S(2)}, u32[]{:S(2)}) %collective-permute-start.8) | collective-permute-done | bytes 393248 | tf_op jit(solution)/shard_map/ppermute | solution.py:24
  65.2 6.8 %collective-permute-done.12.from3 = bf16[768,256]{1,0:T(8,128)(2,1)S(1)} collective-permute-done((bf16[768,256]{1,0:T(8,128)(2,1)S(1)}, bf16[768,256]{1,0:T(8,128)(2,1)S(1)}, u32[]{:S(2)}, u32[]{:S(2)}) %collective-permute-start.12) | collective-permute-done | bytes 393248 | tf_op jit(solution)/shard_map/ppermute | solution.py:24
  72.0 9.3 %update.1 = (bf16[1536,1024]{1,0:T(8,128)(2,1)}, bf16[1536,1024]{1,0:T(8,128)(2,1)}, bf16[16,24,1024]{2,1,0:T(8,128)(2,1)S(1)}, bf16[16,24,1024]{2,1,0:T(8,128)(2,1)S(1)}) custom-call(s32[2,3]{1,0:T(2,128)S(1)} %copy-done.3, s32[2]{0:T(128)S(1)} %copy-done.6, bf16[2,3,768,768]{3,2,1,0:T(8,128)(2,1)S(1)} %get-tuple-element.63.far, ...), custom_call_target="tpu_custom_call" | custom-call | flops 7549747200 | bytes 6291456 | tf_op jit(solution)/shard_map/update/pallas_call | solution.py:304
  81.6 2.2 %collective-permute-done.17 = bf16[16,24,1024]{2,1,0:T(8,128)(2,1)S(1)} collective-permute-done((bf16[16,24,1024]{2,1,0:T(8,128)(2,1)S(1)}, bf16[16,24,1024]{2,1,0:T(8,128)(2,1)S(1)}, u32[]{:S(2)}, u32[]{:S(2)}) %collective-permute-start.17) | collective-permute-done | bytes 786464 | tf_op jit(solution)/shard_map/ppermute | solution.py:24
  87.2 4.8 %collective-permute-done.20 = bf16[4,24,1024]{2,1,0:T(8,128)(2,1)S(1)} collective-permute-done((bf16[4,24,1024]{2,1,0:T(8,128)(2,1)S(1)}, bf16[4,24,1024]{2,1,0:T(8,128)(2,1)S(1)}, u32[]{:S(2)}, u32[]{:S(2)}) %collective-permute-start.20) | collective-permute-done | bytes 196640 | tf_op jit(solution)/shard_map/ppermute | solution.py:24
  91.9 2.1 %collective-permute-done.19 = bf16[4,24,1024]{2,1,0:T(8,128)(2,1)S(1)} collective-permute-done((bf16[4,24,1024]{2,1,0:T(8,128)(2,1)S(1)}, bf16[4,24,1024]{2,1,0:T(8,128)(2,1)S(1)}, u32[]{:S(2)}, u32[]{:S(2)}) %collective-permute-start.19) | collective-permute-done | bytes 196640 | tf_op jit(solution)/shard_map/ppermute | solution.py:24
  94.0 3.0 %collective-permute-done.18 = bf16[4,24,1024]{2,1,0:T(8,128)(2,1)S(1)} collective-permute-done((bf16[4,24,1024]{2,1,0:T(8,128)(2,1)S(1)}, bf16[4,24,1024]{2,1,0:T(8,128)(2,1)S(1)}, u32[]{:S(2)}, u32[]{:S(2)}) %collective-permute-start.18) | collective-permute-done | bytes 196640 | tf_op jit(solution)/shard_map/ppermute | solution.py:24
  97.2 3.4 %collective-permute-start.23 = (bf16[24,1024]{1,0:T(8,128)(2,1)S(1)}, bf16[24,1024]{1,0:T(8,128)(2,1)S(1)}, u32[]{:S(2)}, u32[]{:S(2)}) collective-permute-start(bf16[24,1024]{1,0:T(8,128)(2,1)S(1)} %get-tuple-element.97), channel_id=1, source_target_pairs={{0,24},{1,25},{2,26},{3,27},{4,28},{5,29},{6,30},{7,31},{8,0},{9,1... | collective-permute-start | bytes 147464 | tf_op jit(solution)/shard_map/ppermute | solution.py:24
  102.8 3.4 %collective-permute-done.22 = bf16[24,1024]{1,0:T(8,128)(2,1)S(1)} collective-permute-done((bf16[24,1024]{1,0:T(8,128)(2,1)S(1)}, bf16[24,1024]{1,0:T(8,128)(2,1)S(1)}, u32[]{:S(2)}, u32[]{:S(2)}) %collective-permute-start.22) | collective-permute-done | bytes 49184 | tf_op jit(solution)/shard_map/ppermute | solution.py:24
  111.0 1.8 %collective-permute-done.25 = bf16[24,1024]{1,0:T(8,128)(2,1)S(1)} collective-permute-done((bf16[24,1024]{1,0:T(8,128)(2,1)S(1)}, bf16[24,1024]{1,0:T(8,128)(2,1)S(1)}, u32[]{:S(2)}, u32[]{:S(2)}) %collective-permute-start.25) | collective-permute-done | bytes 49184 | tf_op jit(solution)/shard_map/ppermute | solution.py:24
  (62 shorter events, 26.0 us)
Async XLA Ops:
  0.6 6.8 %collective-permute-start = (s32[1,4]{1,0:T(1,128)}, s32[1,4]{1,0:T(1,128)S(1)}, u32[]{:S(2)}, u32[]{:S(2)}) collective-permute-start(s32[1,4]{1,0:T(1,128)} %request.3), channel_id=1, source_target_pairs={{0,32},{32,64},{64,96},{96,0},{1,33},{33,65},{65,97},{97,1},{2,34}... | collective-permute-start | bytes 56 | tf_op jit(solution)/shard_map/ppermute | solution.py:24
  2.3 5.2 %collective-permute-start.1 = (s32[1,4]{1,0:T(1,128)}, s32[1,4]{1,0:T(1,128)S(1)}, u32[]{:S(2)}, u32[]{:S(2)}) collective-permute-start(s32[1,4]{1,0:T(1,128)} %request.3), channel_id=1, source_target_pairs={{0,64},{32,96},{64,0},{96,32},{1,65},{33,97},{65,1},{97,33},{2,66}... | collective-permute-start | bytes 56 | tf_op jit(solution)/shard_map/ppermute | solution.py:24
  8.7 20.8 %collective-permute-start.9 = (bf16[2,768,128]{2,1,0:T(8,128)(2,1)S(1)}, bf16[2,768,128]{2,1,0:T(8,128)(2,1)S(1)}, u32[]{:S(2)}, u32[]{:S(2)}) collective-permute-start(bf16[2,768,128]{2,1,0:T(8,128)(2,1)S(1)} %slice.3), channel_id=1, source_target_pairs={{0,64},{32,96},{64,0},{96,32},{1,65},{33,97},{65,1},{97,33},{2,66}... | collective-permute-start | bytes 1179656 | tf_op jit(solution)/shard_map/ppermute | solution.py:24
  10.2 6.1 %collective-permute-start.3 = (bf16[24,1024]{1,0:T(8,128)(2,1)}, bf16[24,1024]{1,0:T(8,128)(2,1)S(1)}, u32[]{:S(2)}, u32[]{:S(2)}) collective-permute-start(bf16[24,1024]{1,0:T(8,128)(2,1)} %refs_0_), channel_id=1, source_target_pairs={{0,6},{1,7},{2,0},{3,1},{4,2},{5,3},{6,4},{7,5},{8,14},{9,15},{10,... | collective-permute-start | bytes 147464 | tf_op jit(solution)/shard_map/ppermute | solution.py:24
  14.2 5.9 %collective-permute-start.4 = (bf16[24,1024]{1,0:T(8,128)(2,1)}, bf16[24,1024]{1,0:T(8,128)(2,1)S(1)}, u32[]{:S(2)}, u32[]{:S(2)}) collective-permute-start(bf16[24,1024]{1,0:T(8,128)(2,1)} %refs_0_), channel_id=1, source_target_pairs={{0,4},{1,5},{2,6},{3,7},{4,0},{5,1},{6,2},{7,3},{8,12},{9,13},{10,... | collective-permute-start | bytes 147464 | tf_op jit(solution)/shard_map/ppermute | solution.py:24
  14.2 6.0 %collective-permute-start.5 = (bf16[24,1024]{1,0:T(8,128)(2,1)}, bf16[24,1024]{1,0:T(8,128)(2,1)S(1)}, u32[]{:S(2)}, u32[]{:S(2)}) collective-permute-start(bf16[24,1024]{1,0:T(8,128)(2,1)} %refs_0_), channel_id=1, source_target_pairs={{0,2},{1,3},{2,4},{3,5},{4,6},{5,7},{6,0},{7,1},{8,10},{9,11},{10,... | collective-permute-start | bytes 147464 | tf_op jit(solution)/shard_map/ppermute | solution.py:24
  23.6 20.7 %collective-permute-start.6 = (bf16[768,512]{1,0:T(8,128)(2,1)S(1)}, bf16[768,512]{1,0:T(8,128)(2,1)S(1)}, u32[]{:S(2)}, u32[]{:S(2)}) collective-permute-start(bf16[768,512]{1,0:T(8,128)(2,1)S(1)} %get-tuple-element.66), channel_id=1, source_target_pairs={{0,96},{32,0},{64,32},{96,64},{1,97},{33,1},{65,33},{97,65},{2,98}... | collective-permute-start | bytes 2359304 | tf_op jit(solution)/shard_map/ppermute | solution.py:24
  25.5 26.0 %collective-permute-start.7 = (bf16[768,512]{1,0:T(8,128)(2,1)S(1)}, bf16[768,512]{1,0:T(8,128)(2,1)S(1)}, u32[]{:S(2)}, u32[]{:S(2)}) collective-permute-start(bf16[768,512]{1,0:T(8,128)(2,1)S(1)} %get-tuple-element.67), channel_id=1, source_target_pairs={{0,32},{32,64},{64,96},{96,0},{1,33},{33,65},{65,97},{97,1},{2,34}... | collective-permute-start | bytes 2359304 | tf_op jit(solution)/shard_map/ppermute | solution.py:24
  25.8 8.6 %collective-permute-start.13 = (bf16[4,24,1024]{2,1,0:T(8,128)(2,1)S(1)}, bf16[4,24,1024]{2,1,0:T(8,128)(2,1)S(1)}, u32[]{:S(2)}, u32[]{:S(2)}) collective-permute-start(bf16[4,24,1024]{2,1,0:T(8,128)(2,1)S(1)} %rows_of_z.1.refs_0_), channel_id=1, source_target_pairs={{0,24},{1,25},{2,26},{3,27},{4,28},{5,29},{6,30},{7,31},{8,0},{9,1... | collective-permute-start | bytes 589832 | tf_op jit(solution)/shard_map/ppermute | solution.py:24
  29.1 15.1 %collective-permute-start.14 = (bf16[4,24,1024]{2,1,0:T(8,128)(2,1)S(1)}, bf16[4,24,1024]{2,1,0:T(8,128)(2,1)S(1)}, u32[]{:S(2)}, u32[]{:S(2)}) collective-permute-start(bf16[4,24,1024]{2,1,0:T(8,128)(2,1)S(1)} %rows_of_z.1.refs_0_), channel_id=1, source_target_pairs={{0,16},{1,17},{2,18},{3,19},{4,20},{5,21},{6,22},{7,23},{8,24},{9,... | collective-permute-start | bytes 589832 | tf_op jit(solution)/shard_map/ppermute | solution.py:24
  29.5 14.7 %collective-permute-start.15 = (bf16[4,24,1024]{2,1,0:T(8,128)(2,1)S(1)}, bf16[4,24,1024]{2,1,0:T(8,128)(2,1)S(1)}, u32[]{:S(2)}, u32[]{:S(2)}) collective-permute-start(bf16[4,24,1024]{2,1,0:T(8,128)(2,1)S(1)} %rows_of_z.1.refs_0_), channel_id=1, source_target_pairs={{0,8},{1,9},{2,10},{3,11},{4,12},{5,13},{6,14},{7,15},{8,16},{9,17... | collective-permute-start | bytes 589832 | tf_op jit(solution)/shard_map/ppermute | solution.py:24
  34.4 24.4 %collective-permute-start.10 = (bf16[768,384]{1,0:T(8,128)(2,1)S(1)}, bf16[768,384]{1,0:T(8,128)(2,1)S(1)}, u32[]{:S(2)}, u32[]{:S(2)}) collective-permute-start(bf16[768,384]{1,0:T(8,128)(2,1)S(1)} %get-tuple-element.72), channel_id=1, source_target_pairs={{0,64},{32,96},{64,0},{96,32},{1,65},{33,97},{65,1},{97,33},{2,66}... | collective-permute-start | bytes 1769480 | tf_op jit(solution)/shard_map/ppermute | solution.py:24
  44.3 18.5 %collective-permute-start.16 = (bf16[16,24,1024]{2,1,0:T(8,128)(2,1)S(1)}, bf16[16,24,1024]{2,1,0:T(8,128)(2,1)S(1)}, u32[]{:S(2)}, u32[]{:S(2)}) collective-permute-start(bf16[16,24,1024]{2,1,0:T(8,128)(2,1)S(1)} %bitcast.30), channel_id=1, source_target_pairs={{0,1},{1,0},{2,3},{3,2},{4,5},{5,4},{6,7},{7,6},{8,9},{9,8},{10,11... | collective-permute-start | bytes 2359304 | tf_op jit(solution)/shard_map/ppermute | solution.py:24
  51.5 13.8 %collective-permute-start.8 = (bf16[768,256]{1,0:T(8,128)(2,1)S(1)}, bf16[768,256]{1,0:T(8,128)(2,1)S(1)}, u32[]{:S(2)}, u32[]{:S(2)}) collective-permute-start(bf16[768,256]{1,0:T(8,128)(2,1)S(1)} %get-tuple-element.68), channel_id=1, source_target_pairs={{0,96},{32,0},{64,32},{96,64},{1,97},{33,1},{65,33},{97,65},{2,98}... | collective-permute-start | bytes 1179656 | tf_op jit(solution)/shard_map/ppermute | solution.py:24
  51.5 20.5 %collective-permute-start.12 = (bf16[768,256]{1,0:T(8,128)(2,1)S(1)}, bf16[768,256]{1,0:T(8,128)(2,1)S(1)}, u32[]{:S(2)}, u32[]{:S(2)}) collective-permute-start(bf16[768,256]{1,0:T(8,128)(2,1)S(1)} %get-tuple-element.74), channel_id=1, source_target_pairs={{0,32},{32,64},{64,96},{96,0},{1,33},{33,65},{65,97},{97,1},{2,34}... | collective-permute-start | bytes 1179656 | tf_op jit(solution)/shard_map/ppermute | solution.py:24
  58.9 13.2 %collective-permute-start.11 = (bf16[768,256]{1,0:T(8,128)(2,1)S(1)}, bf16[768,256]{1,0:T(8,128)(2,1)S(1)}, u32[]{:S(2)}, u32[]{:S(2)}) collective-permute-start(bf16[768,256]{1,0:T(8,128)(2,1)S(1)} %get-tuple-element.73), channel_id=1, source_target_pairs={{0,64},{32,96},{64,0},{96,32},{1,65},{33,97},{65,1},{97,33},{2,66}... | collective-permute-start | bytes 1179656 | tf_op jit(solution)/shard_map/ppermute | solution.py:24
  84.1 7.8 %collective-permute-start.20 = (bf16[4,24,1024]{2,1,0:T(8,128)(2,1)S(1)}, bf16[4,24,1024]{2,1,0:T(8,128)(2,1)S(1)}, u32[]{:S(2)}, u32[]{:S(2)}) collective-permute-start(bf16[4,24,1024]{2,1,0:T(8,128)(2,1)S(1)} %get-tuple-element.94), channel_id=1, source_target_pairs={{0,6},{1,7},{2,0},{3,1},{4,2},{5,3},{6,4},{7,5},{8,14},{9,15},{10,... | collective-permute-start | bytes 589832 | tf_op jit(solution)/shard_map/ppermute | solution.py:24
  84.7 9.3 %collective-permute-start.19 = (bf16[4,24,1024]{2,1,0:T(8,128)(2,1)S(1)}, bf16[4,24,1024]{2,1,0:T(8,128)(2,1)S(1)}, u32[]{:S(2)}, u32[]{:S(2)}) collective-permute-start(bf16[4,24,1024]{2,1,0:T(8,128)(2,1)S(1)} %get-tuple-element.95), channel_id=1, source_target_pairs={{0,4},{1,5},{2,6},{3,7},{4,0},{5,1},{6,2},{7,3},{8,12},{9,13},{10,... | collective-permute-start | bytes 589832 | tf_op jit(solution)/shard_map/ppermute | solution.py:24
  85.8 11.2 %collective-permute-start.18 = (bf16[4,24,1024]{2,1,0:T(8,128)(2,1)S(1)}, bf16[4,24,1024]{2,1,0:T(8,128)(2,1)S(1)}, u32[]{:S(2)}, u32[]{:S(2)}) collective-permute-start(bf16[4,24,1024]{2,1,0:T(8,128)(2,1)S(1)} %get-tuple-element.93), channel_id=1, source_target_pairs={{0,2},{1,3},{2,4},{3,5},{4,6},{5,7},{6,0},{7,1},{8,10},{9,11},{10,... | collective-permute-start | bytes 589832 | tf_op jit(solution)/shard_map/ppermute | solution.py:24
  97.2 5.6 %collective-permute-start.23 = (bf16[24,1024]{1,0:T(8,128)(2,1)S(1)}, bf16[24,1024]{1,0:T(8,128)(2,1)S(1)}, u32[]{:S(2)}, u32[]{:S(2)}) collective-permute-start(bf16[24,1024]{1,0:T(8,128)(2,1)S(1)} %get-tuple-element.97), channel_id=1, source_target_pairs={{0,24},{1,25},{2,26},{3,27},{4,28},{5,29},{6,30},{7,31},{8,0},{9,1... | collective-permute-start | bytes 147464 | tf_op jit(solution)/shard_map/ppermute | solution.py:24
  100.6 5.6 %collective-permute-start.22 = (bf16[24,1024]{1,0:T(8,128)(2,1)S(1)}, bf16[24,1024]{1,0:T(8,128)(2,1)S(1)}, u32[]{:S(2)}, u32[]{:S(2)}) collective-permute-start(bf16[24,1024]{1,0:T(8,128)(2,1)S(1)} %get-tuple-element.98), channel_id=1, source_target_pairs={{0,16},{1,17},{2,18},{3,19},{4,20},{5,21},{6,22},{7,23},{8,24},{9,... | collective-permute-start | bytes 147464 | tf_op jit(solution)/shard_map/ppermute | solution.py:24
  101.3 5.5 %collective-permute-start.21 = (bf16[24,1024]{1,0:T(8,128)(2,1)S(1)}, bf16[24,1024]{1,0:T(8,128)(2,1)S(1)}, u32[]{:S(2)}, u32[]{:S(2)}) collective-permute-start(bf16[24,1024]{1,0:T(8,128)(2,1)S(1)} %get-tuple-element.96), channel_id=1, source_target_pairs={{0,8},{1,9},{2,10},{3,11},{4,12},{5,13},{6,14},{7,15},{8,16},{9,17... | collective-permute-start | bytes 147464 | tf_op jit(solution)/shard_map/ppermute | solution.py:24
  107.2 5.6 %collective-permute-start.25 = (bf16[24,1024]{1,0:T(8,128)(2,1)S(1)}, bf16[24,1024]{1,0:T(8,128)(2,1)S(1)}, u32[]{:S(2)}, u32[]{:S(2)}) collective-permute-start(bf16[24,1024]{1,0:T(8,128)(2,1)S(1)} %fusion.5), channel_id=1, source_target_pairs={{0,64},{32,96},{64,0},{96,32},{1,65},{33,97},{65,1},{97,33},{2,66}... | collective-permute-start | bytes 147464 | tf_op jit(solution)/shard_map/ppermute | solution.py:24
  108.7 5.3 %collective-permute-start.24 = (bf16[24,1024]{1,0:T(8,128)(2,1)S(1)}, bf16[24,1024]{1,0:T(8,128)(2,1)S(1)}, u32[]{:S(2)}, u32[]{:S(2)}) collective-permute-start(bf16[24,1024]{1,0:T(8,128)(2,1)S(1)} %fusion.5), channel_id=1, source_target_pairs={{0,32},{32,64},{64,96},{96,0},{1,33},{33,65},{65,97},{97,1},{2,34}... | collective-permute-start | bytes 147464 | tf_op jit(solution)/shard_map/ppermute | solution.py:24
  (12 other events, 85.8 us)

commit v4 on v3

--- a/solution.py
+++ b/solution.py
@@ -376,10 +376,6 @@
     )(mine, other)
 
 
-def weight_of_z(rows):
-    return call_arrange(my_z, [rows] + [along_z(rows, 4 - d) for d in (1, 2, 3)], "rows_of_z")
-
-
 def whole_weight(parts, after):
     piece, hidden = parts.shape[1:]
     rows = [parts] + [along_y(parts, 4 - d) for d in (1, 2, 3)]
@@ -414,9 +410,11 @@
     asks = [along_comm(request, rel) for rel in (1, 2, 3)]
     first, w_rows, *asks = lax.optimization_barrier((feats[:, :, :EARLY], w_rows, *asks))
     early = along_comm(first, 2)
-    of_z, *asks = lax.optimization_barrier((weight_of_z(w_rows), *asks))
+    beside = [along_z(w_rows, 4 - d) for d in (1, 2, 3)]
     chosen = call_choose(asks, feats)
-    tiles, of_z, *chosen = lax.optimization_barrier((tiles, of_z, *chosen))
+    tiles, *both = lax.optimization_barrier((tiles, *beside, *chosen))
+    beside, chosen = both[:3], both[3:]
+    of_z = call_arrange(my_z, [w_rows, *beside], "rows_of_z")
     early, chosen[2] = lax.optimization_barrier((early, chosen[2]))
     heads = [along_comm(chosen[2 * n], 3 - n) for n in range(3)]
     near, far_off = [heads[0], heads[2]], [heads[1]]

time: 115 us -> 113 us (0.983)
  local copies, waits for them, and re-layouts: 3.91 us -> 1.13 us
  starting transfers between devices: 36.4 us -> 35 us
  waiting for transfers between devices: 51.5 us -> 52.9 us
    unnamed x18 -> x14, local copies, waits for them, and re-layouts: 2.82 us -> 0.04 us
    ppermute x27, starting transfers between devices: 36.4 us -> 35 us  [shifted(): return lax.ppermute(x, axis, [(i, to(i)) for i in range(size)])]
    ppermute x27, waiting for transfers between devices: 51.5 us -> 52.9 us  [shifted(): return lax.ppermute(x, axis, [(i, to(i)) for i in range(size)])]
  transfers between devices with their start and end apart: 27 -> 27, of which waited for: 19 -> 19; matrix products, arithmetic and copies ran while one was open for 1% -> 1% of each run, Pallas kernels for 10% -> 11%
where the time goes in v4:
time: 113 us
  waiting for transfers between devices  52.9 us (47%)
  starting transfers between devices  35 us (31%)
  Pallas kernels  21.8 us (19%)
    ppermute x27, waiting for transfers between devices, shifted(): return lax.ppermute(x, axis, [(i, to(i)) for i in range(size)])  52.9 us
    ppermute x27, starting transfers between devices, shifted(): return lax.ppermute(x, axis, [(i, to(i)) for i in range(size)])  35 us
    pallas_call x1, Pallas kernels, call_update(): pl.pallas_call(update, out_shape=(wide, wide, half, half), in_specs=[SMEM...  9.8 us
    pallas_call x1, Pallas kernels, call_own_products(): pl.pallas_call(own_products, out_shape=(jax.ShapeDtypeStruct((comms, node...  5.51 us
    pallas_call x1, Pallas kernels, call_head_products(): pl.pallas_call(head_products, out_shape=jax.ShapeDtypeStruct(acc.shape, a...  3.73 us
    pallas_call x1, Pallas kernels, call_choose(): pl.pallas_call(choose, out_shape=shapes, in_specs=[SMEM] * 3 + [HBM], out...  2.51 us
  transfers between devices with their start and end apart: 27, of which 19 were waited for; matrix products, arithmetic and copies ran while one was open for 1% of the time, Pallas kernels for 11%

profile of v4, /device:TPU:0, one launch (start us, length us, event | category | flops | bytes accessed | tf_op | source)
XLA Modules:
  0.0 112.9 jit_solution(16913927999303737170)
XLA Ops:
  2.3 2.7 %collective-permute-start.1 = (s32[1,4]{1,0:T(1,128)}, s32[1,4]{1,0:T(1,128)S(1)}, u32[]{:S(2)}, u32[]{:S(2)}) collective-permute-start(s32[1,4]{1,0:T(1,128)} %request.3), channel_id=1, source_target_pairs={{0,64},{32,96},{64,0},{96,32},{1,65},{33,97},{65,1},{97,33},{2,66}... | collective-permute-start | bytes 56 | tf_op jit(solution)/shard_map/ppermute | solution.py:24
  10.2 4.0 %collective-permute-start.3 = (bf16[24,1024]{1,0:T(8,128)(2,1)}, bf16[24,1024]{1,0:T(8,128)(2,1)S(1)}, u32[]{:S(2)}, u32[]{:S(2)}) collective-permute-start(bf16[24,1024]{1,0:T(8,128)(2,1)} %refs_0_), channel_id=1, source_target_pairs={{0,6},{1,7},{2,0},{3,1},{4,2},{5,3},{6,4},{7,5},{8,14},{9,15},{10,... | collective-permute-start | bytes 147464 | tf_op jit(solution)/shard_map/ppermute | solution.py:24
  15.5 2.5 %choose.1 = (bf16[768,512]{1,0:T(8,128)(2,1)S(1)}, bf16[768,256]{1,0:T(8,128)(2,1)S(1)}, bf16[768,384]{1,0:T(8,128)(2,1)S(1)}, bf16[768,256]{1,0:T(8,128)(2,1)S(...) custom-call(s32[1,4]{1,0:T(1,128)S(1)} %collective-permute-done.ask1, ...), custom_call_target="tpu_custom_call" | custom-call | flops 1048576 | bytes 65536 | tf_op jit(solution)/shard_map/choose/pallas_call | solution.py:82
  18.1 2.1 %collective-permute-done.4.refs_2_ = bf16[24,1024]{1,0:T(8,128)(2,1)S(1)} collective-permute-done((bf16[24,1024]{1,0:T(8,128)(2,1)}, bf16[24,1024]{1,0:T(8,128)(2,1)S(1)}, u32[]{:S(2)}, u32[]{:S(2)}) %collective-permute-start.4) | collective-permute-done | bytes 49184 | tf_op jit(solution)/shard_map/ppermute | solution.py:24
  22.4 3.1 %collective-permute-start.13 = (bf16[4,24,1024]{2,1,0:T(8,128)(2,1)S(1)}, bf16[4,24,1024]{2,1,0:T(8,128)(2,1)S(1)}, u32[]{:S(2)}, u32[]{:S(2)}) collective-permute-start(bf16[4,24,1024]{2,1,0:T(8,128)(2,1)S(1)} %rows_of_z.1.refs_0_), channel_id=1, source_target_pairs={{0,24},{1,25},{2,26},{3,27},{4,28},{5,29},{6,30},{7,31},{8,0},{9,1... | collective-permute-start | bytes 589832 | tf_op jit(solution)/shard_map/ppermute | solution.py:24
  27.1 3.7 %collective-permute-done.13.refs_1_ = bf16[4,24,1024]{2,1,0:T(8,128)(2,1)S(1)} collective-permute-done((bf16[4,24,1024]{2,1,0:T(8,128)(2,1)S(1)}, bf16[4,24,1024]{2,1,0:T(8,128)(2,1)S(1)}, u32[]{:S(2)}, u32[]{:S(2)}) %collective-permute-start.13) | collective-permute-done | bytes 196640 | tf_op jit(solution)/shard_map/ppermute | solution.py:24
  30.8 2.0 %collective-permute-start.10 = (bf16[768,384]{1,0:T(8,128)(2,1)S(1)}, bf16[768,384]{1,0:T(8,128)(2,1)S(1)}, u32[]{:S(2)}, u32[]{:S(2)}) collective-permute-start(bf16[768,384]{1,0:T(8,128)(2,1)S(1)} %get-tuple-element.66), channel_id=1, source_target_pairs={{0,64},{32,96},{64,0},{96,32},{1,65},{33,97},{65,1},{97,33},{2,66}... | collective-permute-start | bytes 1769480 | tf_op jit(solution)/shard_map/ppermute | solution.py:24
  32.9 5.5 %own_products.1 = (f32[2,768,768]{2,1,0:T(8,128)S(1)}, bf16[2,3,768,768]{3,2,1,0:T(8,128)(2,1)S(1)}, bf16[1536,1024]{1,0:T(8,128)(2,1)S(1)}, bf16[1536,1024]{1,0:T(8,128)(2,1)S(1)}, bf16[1536,1024]{1,0:T(8,128)(2,1)S(1)}) custom-call(s32[2,3]{1,0:T(2,128)S(1)} %copy-done.2, s32[2]{0:T(128)S(1)} %copy-done.4, s32[1,4]{1,0:T(1,128)S(1)} %copy-done.3, ...), custom_call_target="tpu_custom_call" | custom-call | flops 1048576 | bytes 65536 | tf_op jit(solution)/shard_map/own_products/pallas_call | solution.py:155
  38.6 2.2 %collective-permute-done.6.head1 = bf16[768,512]{1,0:T(8,128)(2,1)S(1)} collective-permute-done((bf16[768,512]{1,0:T(8,128)(2,1)S(1)}, bf16[768,512]{1,0:T(8,128)(2,1)S(1)}, u32[]{:S(2)}, u32[]{:S(2)}) %collective-permute-start.6) | collective-permute-done | bytes 786464 | tf_op jit(solution)/shard_map/ppermute | solution.py:24
  40.8 8.4 %collective-permute-done.7.head3 = bf16[768,512]{1,0:T(8,128)(2,1)S(1)} collective-permute-done((bf16[768,512]{1,0:T(8,128)(2,1)S(1)}, bf16[768,512]{1,0:T(8,128)(2,1)S(1)}, u32[]{:S(2)}, u32[]{:S(2)}) %collective-permute-start.7) | collective-permute-done | bytes 786464 | tf_op jit(solution)/shard_map/ppermute | solution.py:24
  49.2 2.0 %collective-permute-start.12 = (bf16[768,256]{1,0:T(8,128)(2,1)S(1)}, bf16[768,256]{1,0:T(8,128)(2,1)S(1)}, u32[]{:S(2)}, u32[]{:S(2)}) collective-permute-start(bf16[768,256]{1,0:T(8,128)(2,1)S(1)} %get-tuple-element.68), channel_id=1, source_target_pairs={{0,32},{32,64},{64,96},{96,0},{1,33},{33,65},{65,97},{97,1},{2,34}... | collective-permute-start | bytes 1179656 | tf_op jit(solution)/shard_map/ppermute | solution.py:24
  51.2 4.4 %collective-permute-done.10.head2 = bf16[768,384]{1,0:T(8,128)(2,1)S(1)} collective-permute-done((bf16[768,384]{1,0:T(8,128)(2,1)S(1)}, bf16[768,384]{1,0:T(8,128)(2,1)S(1)}, u32[]{:S(2)}, u32[]{:S(2)}) %collective-permute-start.10) | collective-permute-done | bytes 589856 | tf_op jit(solution)/shard_map/ppermute | solution.py:24
  57.0 3.7 %head_products.1.acc = f32[2,768,768]{2,1,0:T(8,128)S(1)} custom-call(s32[2,3]{1,0:T(2,128)S(1)} %copy-done.2, s32[2]{0:T(128)S(1)} %copy-done.4, s32[1,4]{1,0:T(1,128)S(1)} %copy-done.3, bf16[2,3,768,768]{3,2,1,0:T(8,128)(2,1)S(1)} %get-tuple-element.57.far, bf16[2,768,128]{2,1,0:T(8,128)(2,1)S(1)} %collective-permute-done.9.early, ...), custom_call_target="tpu_custom_call", output_to_operand_aliasing={{}: (8, {})} | custom-call | flops 1048576 | bytes 65536 | tf_op jit(solution)/shard_map/head_products/pallas_call | solution.py:208
  61.9 6.7 %collective-permute-done.12.from3 = bf16[768,256]{1,0:T(8,128)(2,1)S(1)} collective-permute-done((bf16[768,256]{1,0:T(8,128)(2,1)S(1)}, bf16[768,256]{1,0:T(8,128)(2,1)S(1)}, u32[]{:S(2)}, u32[]{:S(2)}) %collective-permute-start.12) | collective-permute-done | bytes 393248 | tf_op jit(solution)/shard_map/ppermute | solution.py:24
  68.6 9.8 %update.1 = (bf16[1536,1024]{1,0:T(8,128)(2,1)}, bf16[1536,1024]{1,0:T(8,128)(2,1)}, bf16[16,24,1024]{2,1,0:T(8,128)(2,1)S(1)}, bf16[16,24,1024]{2,1,0:T(8,128)(2,1)S(1)}) custom-call(s32[2,3]{1,0:T(2,128)S(1)} %copy-done.2, s32[2]{0:T(128)S(1)} %copy-done.4, bf16[2,3,768,768]{3,2,1,0:T(8,128)(2,1)S(1)} %get-tuple-element.57.far, ...), custom_call_target="tpu_custom_call" | custom-call | flops 7549747200 | bytes 6291456 | tf_op jit(solution)/shard_map/update/pallas_call | solution.py:304
  78.6 2.2 %collective-permute-done.17 = bf16[16,24,1024]{2,1,0:T(8,128)(2,1)S(1)} collective-permute-done((bf16[16,24,1024]{2,1,0:T(8,128)(2,1)S(1)}, bf16[16,24,1024]{2,1,0:T(8,128)(2,1)S(1)}, u32[]{:S(2)}, u32[]{:S(2)}) %collective-permute-start.17) | collective-permute-done | bytes 786464 | tf_op jit(solution)/shard_map/ppermute | solution.py:24
  83.9 5.1 %collective-permute-done.20 = bf16[4,24,1024]{2,1,0:T(8,128)(2,1)S(1)} collective-permute-done((bf16[4,24,1024]{2,1,0:T(8,128)(2,1)S(1)}, bf16[4,24,1024]{2,1,0:T(8,128)(2,1)S(1)}, u32[]{:S(2)}, u32[]{:S(2)}) %collective-permute-start.20) | collective-permute-done | bytes 196640 | tf_op jit(solution)/shard_map/ppermute | solution.py:24
  89.0 2.8 %collective-permute-done.19 = bf16[4,24,1024]{2,1,0:T(8,128)(2,1)S(1)} collective-permute-done((bf16[4,24,1024]{2,1,0:T(8,128)(2,1)S(1)}, bf16[4,24,1024]{2,1,0:T(8,128)(2,1)S(1)}, u32[]{:S(2)}, u32[]{:S(2)}) %collective-permute-start.19) | collective-permute-done | bytes 196640 | tf_op jit(solution)/shard_map/ppermute | solution.py:24
  91.8 3.0 %collective-permute-done.18 = bf16[4,24,1024]{2,1,0:T(8,128)(2,1)S(1)} collective-permute-done((bf16[4,24,1024]{2,1,0:T(8,128)(2,1)S(1)}, bf16[4,24,1024]{2,1,0:T(8,128)(2,1)S(1)}, u32[]{:S(2)}, u32[]{:S(2)}) %collective-permute-start.18) | collective-permute-done | bytes 196640 | tf_op jit(solution)/shard_map/ppermute | solution.py:24
  95.0 2.3 %collective-permute-start.23 = (bf16[24,1024]{1,0:T(8,128)(2,1)S(1)}, bf16[24,1024]{1,0:T(8,128)(2,1)S(1)}, u32[]{:S(2)}, u32[]{:S(2)}) collective-permute-start(bf16[24,1024]{1,0:T(8,128)(2,1)S(1)} %get-tuple-element.93), channel_id=1, source_target_pairs={{0,24},{1,25},{2,26},{3,27},{4,28},{5,29},{6,30},{7,31},{8,0},{9,1... | collective-permute-start | bytes 147464 | tf_op jit(solution)/shard_map/ppermute | solution.py:24
  97.3 1.6 %collective-permute-start.22 = (bf16[24,1024]{1,0:T(8,128)(2,1)S(1)}, bf16[24,1024]{1,0:T(8,128)(2,1)S(1)}, u32[]{:S(2)}, u32[]{:S(2)}) collective-permute-start(bf16[24,1024]{1,0:T(8,128)(2,1)S(1)} %get-tuple-element.94), channel_id=1, source_target_pairs={{0,16},{1,17},{2,18},{3,19},{4,20},{5,21},{6,22},{7,23},{8,24},{9,... | collective-permute-start | bytes 147464 | tf_op jit(solution)/shard_map/ppermute | solution.py:24
  99.3 3.7 %collective-permute-done.22 = bf16[24,1024]{1,0:T(8,128)(2,1)S(1)} collective-permute-done((bf16[24,1024]{1,0:T(8,128)(2,1)S(1)}, bf16[24,1024]{1,0:T(8,128)(2,1)S(1)}, u32[]{:S(2)}, u32[]{:S(2)}) %collective-permute-start.22) | collective-permute-done | bytes 49184 | tf_op jit(solution)/shard_map/ppermute | solution.py:24
  104.3 2.2 %collective-permute-start.26 = (bf16[24,1024]{1,0:T(8,128)(2,1)S(1)}, bf16[24,1024]{1,0:T(8,128)(2,1)S(1)}, u32[]{:S(2)}, u32[]{:S(2)}) collective-permute-start(bf16[24,1024]{1,0:T(8,128)(2,1)S(1)} %fusion.5), channel_id=1, source_target_pairs={{0,96},{32,0},{64,32},{96,64},{1,97},{33,1},{65,33},{97,65},{2,98}... | collective-permute-start | bytes 147464 | tf_op jit(solution)/shard_map/ppermute | solution.py:24
  108.4 3.7 %collective-permute-done.25 = bf16[24,1024]{1,0:T(8,128)(2,1)S(1)} collective-permute-done((bf16[24,1024]{1,0:T(8,128)(2,1)S(1)}, bf16[24,1024]{1,0:T(8,128)(2,1)S(1)}, u32[]{:S(2)}, u32[]{:S(2)}) %collective-permute-start.25) | collective-permute-done | bytes 49184 | tf_op jit(solution)/shard_map/ppermute | solution.py:24
  (58 shorter events, 22.4 us)
Async XLA Ops:
  0.7 6.8 %collective-permute-start = (s32[1,4]{1,0:T(1,128)}, s32[1,4]{1,0:T(1,128)S(1)}, u32[]{:S(2)}, u32[]{:S(2)}) collective-permute-start(s32[1,4]{1,0:T(1,128)} %request.3), channel_id=1, source_target_pairs={{0,32},{32,64},{64,96},{96,0},{1,33},{33,65},{65,97},{97,1},{2,34}... | collective-permute-start | bytes 56 | tf_op jit(solution)/shard_map/ppermute | solution.py:24
  2.3 5.2 %collective-permute-start.1 = (s32[1,4]{1,0:T(1,128)}, s32[1,4]{1,0:T(1,128)S(1)}, u32[]{:S(2)}, u32[]{:S(2)}) collective-permute-start(s32[1,4]{1,0:T(1,128)} %request.3), channel_id=1, source_target_pairs={{0,64},{32,96},{64,0},{96,32},{1,65},{33,97},{65,1},{97,33},{2,66}... | collective-permute-start | bytes 56 | tf_op jit(solution)/shard_map/ppermute | solution.py:24
  8.7 17.4 %collective-permute-start.9 = (bf16[2,768,128]{2,1,0:T(8,128)(2,1)S(1)}, bf16[2,768,128]{2,1,0:T(8,128)(2,1)S(1)}, u32[]{:S(2)}, u32[]{:S(2)}) collective-permute-start(bf16[2,768,128]{2,1,0:T(8,128)(2,1)S(1)} %slice.3), channel_id=1, source_target_pairs={{0,64},{32,96},{64,0},{96,32},{1,65},{33,97},{65,1},{97,33},{2,66}... | collective-permute-start | bytes 1179656 | tf_op jit(solution)/shard_map/ppermute | solution.py:24
  10.2 7.8 %collective-permute-start.3 = (bf16[24,1024]{1,0:T(8,128)(2,1)}, bf16[24,1024]{1,0:T(8,128)(2,1)S(1)}, u32[]{:S(2)}, u32[]{:S(2)}) collective-permute-start(bf16[24,1024]{1,0:T(8,128)(2,1)} %refs_0_), channel_id=1, source_target_pairs={{0,6},{1,7},{2,0},{3,1},{4,2},{5,3},{6,4},{7,5},{8,14},{9,15},{10,... | collective-permute-start | bytes 147464 | tf_op jit(solution)/shard_map/ppermute | solution.py:24
  14.3 5.9 %collective-permute-start.4 = (bf16[24,1024]{1,0:T(8,128)(2,1)}, bf16[24,1024]{1,0:T(8,128)(2,1)S(1)}, u32[]{:S(2)}, u32[]{:S(2)}) collective-permute-start(bf16[24,1024]{1,0:T(8,128)(2,1)} %refs_0_), channel_id=1, source_target_pairs={{0,4},{1,5},{2,6},{3,7},{4,0},{5,1},{6,2},{7,3},{8,12},{9,13},{10,... | collective-permute-start | bytes 147464 | tf_op jit(solution)/shard_map/ppermute | solution.py:24
  14.3 6.0 %collective-permute-start.5 = (bf16[24,1024]{1,0:T(8,128)(2,1)}, bf16[24,1024]{1,0:T(8,128)(2,1)S(1)}, u32[]{:S(2)}, u32[]{:S(2)}) collective-permute-start(bf16[24,1024]{1,0:T(8,128)(2,1)} %refs_0_), channel_id=1, source_target_pairs={{0,2},{1,3},{2,4},{3,5},{4,6},{5,7},{6,0},{7,1},{8,10},{9,11},{10,... | collective-permute-start | bytes 147464 | tf_op jit(solution)/shard_map/ppermute | solution.py:24
  20.3 20.5 %collective-permute-start.6 = (bf16[768,512]{1,0:T(8,128)(2,1)S(1)}, bf16[768,512]{1,0:T(8,128)(2,1)S(1)}, u32[]{:S(2)}, u32[]{:S(2)}) collective-permute-start(bf16[768,512]{1,0:T(8,128)(2,1)S(1)} %get-tuple-element.60), channel_id=1, source_target_pairs={{0,96},{32,0},{64,32},{96,64},{1,97},{33,1},{65,33},{97,65},{2,98}... | collective-permute-start | bytes 2359304 | tf_op jit(solution)/shard_map/ppermute | solution.py:24
  21.8 27.4 %collective-permute-start.7 = (bf16[768,512]{1,0:T(8,128)(2,1)S(1)}, bf16[768,512]{1,0:T(8,128)(2,1)S(1)}, u32[]{:S(2)}, u32[]{:S(2)}) collective-permute-start(bf16[768,512]{1,0:T(8,128)(2,1)S(1)} %get-tuple-element.61), channel_id=1, source_target_pairs={{0,32},{32,64},{64,96},{96,0},{1,33},{33,65},{65,97},{97,1},{2,34}... | collective-permute-start | bytes 2359304 | tf_op jit(solution)/shard_map/ppermute | solution.py:24
  22.4 8.4 %collective-permute-start.13 = (bf16[4,24,1024]{2,1,0:T(8,128)(2,1)S(1)}, bf16[4,24,1024]{2,1,0:T(8,128)(2,1)S(1)}, u32[]{:S(2)}, u32[]{:S(2)}) collective-permute-start(bf16[4,24,1024]{2,1,0:T(8,128)(2,1)S(1)} %rows_of_z.1.refs_0_), channel_id=1, source_target_pairs={{0,24},{1,25},{2,26},{3,27},{4,28},{5,29},{6,30},{7,31},{8,0},{9,1... | collective-permute-start | bytes 589832 | tf_op jit(solution)/shard_map/ppermute | solution.py:24
  25.5 12.9 %collective-permute-start.14 = (bf16[4,24,1024]{2,1,0:T(8,128)(2,1)S(1)}, bf16[4,24,1024]{2,1,0:T(8,128)(2,1)S(1)}, u32[]{:S(2)}, u32[]{:S(2)}) collective-permute-start(bf16[4,24,1024]{2,1,0:T(8,128)(2,1)S(1)} %rows_of_z.1.refs_0_), channel_id=1, source_target_pairs={{0,16},{1,17},{2,18},{3,19},{4,20},{5,21},{6,22},{7,23},{8,24},{9,... | collective-permute-start | bytes 589832 | tf_op jit(solution)/shard_map/ppermute | solution.py:24
  26.1 12.3 %collective-permute-start.15 = (bf16[4,24,1024]{2,1,0:T(8,128)(2,1)S(1)}, bf16[4,24,1024]{2,1,0:T(8,128)(2,1)S(1)}, u32[]{:S(2)}, u32[]{:S(2)}) collective-permute-start(bf16[4,24,1024]{2,1,0:T(8,128)(2,1)S(1)} %rows_of_z.1.refs_0_), channel_id=1, source_target_pairs={{0,8},{1,9},{2,10},{3,11},{4,12},{5,13},{6,14},{7,15},{8,16},{9,17... | collective-permute-start | bytes 589832 | tf_op jit(solution)/shard_map/ppermute | solution.py:24
  30.8 24.8 %collective-permute-start.10 = (bf16[768,384]{1,0:T(8,128)(2,1)S(1)}, bf16[768,384]{1,0:T(8,128)(2,1)S(1)}, u32[]{:S(2)}, u32[]{:S(2)}) collective-permute-start(bf16[768,384]{1,0:T(8,128)(2,1)S(1)} %get-tuple-element.66), channel_id=1, source_target_pairs={{0,64},{32,96},{64,0},{96,32},{1,65},{33,97},{65,1},{97,33},{2,66}... | collective-permute-start | bytes 1769480 | tf_op jit(solution)/shard_map/ppermute | solution.py:24
  38.5 22.3 %collective-permute-start.16 = (bf16[16,24,1024]{2,1,0:T(8,128)(2,1)S(1)}, bf16[16,24,1024]{2,1,0:T(8,128)(2,1)S(1)}, u32[]{:S(2)}, u32[]{:S(2)}) collective-permute-start(bf16[16,24,1024]{2,1,0:T(8,128)(2,1)S(1)} %bitcast.30), channel_id=1, source_target_pairs={{0,1},{1,0},{2,3},{3,2},{4,5},{5,4},{6,7},{7,6},{8,9},{9,8},{10,11... | collective-permute-start | bytes 2359304 | tf_op jit(solution)/shard_map/ppermute | solution.py:24
  49.2 12.7 %collective-permute-start.8 = (bf16[768,256]{1,0:T(8,128)(2,1)S(1)}, bf16[768,256]{1,0:T(8,128)(2,1)S(1)}, u32[]{:S(2)}, u32[]{:S(2)}) collective-permute-start(bf16[768,256]{1,0:T(8,128)(2,1)S(1)} %get-tuple-element.62), channel_id=1, source_target_pairs={{0,96},{32,0},{64,32},{96,64},{1,97},{33,1},{65,33},{97,65},{2,98}... | collective-permute-start | bytes 1179656 | tf_op jit(solution)/shard_map/ppermute | solution.py:24
  49.2 19.4 %collective-permute-start.12 = (bf16[768,256]{1,0:T(8,128)(2,1)S(1)}, bf16[768,256]{1,0:T(8,128)(2,1)S(1)}, u32[]{:S(2)}, u32[]{:S(2)}) collective-permute-start(bf16[768,256]{1,0:T(8,128)(2,1)S(1)} %get-tuple-element.68), channel_id=1, source_target_pairs={{0,32},{32,64},{64,96},{96,0},{1,33},{33,65},{65,97},{97,1},{2,34}... | collective-permute-start | bytes 1179656 | tf_op jit(solution)/shard_map/ppermute | solution.py:24
  55.6 13.0 %collective-permute-start.11 = (bf16[768,256]{1,0:T(8,128)(2,1)S(1)}, bf16[768,256]{1,0:T(8,128)(2,1)S(1)}, u32[]{:S(2)}, u32[]{:S(2)}) collective-permute-start(bf16[768,256]{1,0:T(8,128)(2,1)S(1)} %get-tuple-element.67), channel_id=1, source_target_pairs={{0,64},{32,96},{64,0},{96,32},{1,65},{33,97},{65,1},{97,33},{2,66}... | collective-permute-start | bytes 1179656 | tf_op jit(solution)/shard_map/ppermute | solution.py:24
  81.2 7.8 %collective-permute-start.20 = (bf16[4,24,1024]{2,1,0:T(8,128)(2,1)S(1)}, bf16[4,24,1024]{2,1,0:T(8,128)(2,1)S(1)}, u32[]{:S(2)}, u32[]{:S(2)}) collective-permute-start(bf16[4,24,1024]{2,1,0:T(8,128)(2,1)S(1)} %get-tuple-element.90), channel_id=1, source_target_pairs={{0,6},{1,7},{2,0},{3,1},{4,2},{5,3},{6,4},{7,5},{8,14},{9,15},{10,... | collective-permute-start | bytes 589832 | tf_op jit(solution)/shard_map/ppermute | solution.py:24
  82.5 9.3 %collective-permute-start.19 = (bf16[4,24,1024]{2,1,0:T(8,128)(2,1)S(1)}, bf16[4,24,1024]{2,1,0:T(8,128)(2,1)S(1)}, u32[]{:S(2)}, u32[]{:S(2)}) collective-permute-start(bf16[4,24,1024]{2,1,0:T(8,128)(2,1)S(1)} %get-tuple-element.91), channel_id=1, source_target_pairs={{0,4},{1,5},{2,6},{3,7},{4,0},{5,1},{6,2},{7,3},{8,12},{9,13},{10,... | collective-permute-start | bytes 589832 | tf_op jit(solution)/shard_map/ppermute | solution.py:24
  83.1 11.8 %collective-permute-start.18 = (bf16[4,24,1024]{2,1,0:T(8,128)(2,1)S(1)}, bf16[4,24,1024]{2,1,0:T(8,128)(2,1)S(1)}, u32[]{:S(2)}, u32[]{:S(2)}) collective-permute-start(bf16[4,24,1024]{2,1,0:T(8,128)(2,1)S(1)} %get-tuple-element.89), channel_id=1, source_target_pairs={{0,2},{1,3},{2,4},{3,5},{4,6},{5,7},{6,0},{7,1},{8,10},{9,11},{10,... | collective-permute-start | bytes 589832 | tf_op jit(solution)/shard_map/ppermute | solution.py:24
  95.0 4.2 %collective-permute-start.23 = (bf16[24,1024]{1,0:T(8,128)(2,1)S(1)}, bf16[24,1024]{1,0:T(8,128)(2,1)S(1)}, u32[]{:S(2)}, u32[]{:S(2)}) collective-permute-start(bf16[24,1024]{1,0:T(8,128)(2,1)S(1)} %get-tuple-element.93), channel_id=1, source_target_pairs={{0,24},{1,25},{2,26},{3,27},{4,28},{5,29},{6,30},{7,31},{8,0},{9,1... | collective-permute-start | bytes 147464 | tf_op jit(solution)/shard_map/ppermute | solution.py:24
  97.3 5.7 %collective-permute-start.22 = (bf16[24,1024]{1,0:T(8,128)(2,1)S(1)}, bf16[24,1024]{1,0:T(8,128)(2,1)S(1)}, u32[]{:S(2)}, u32[]{:S(2)}) collective-permute-start(bf16[24,1024]{1,0:T(8,128)(2,1)S(1)} %get-tuple-element.94), channel_id=1, source_target_pairs={{0,16},{1,17},{2,18},{3,19},{4,20},{5,21},{6,22},{7,23},{8,24},{9,... | collective-permute-start | bytes 147464 | tf_op jit(solution)/shard_map/ppermute | solution.py:24
  98.9 5.3 %collective-permute-start.21 = (bf16[24,1024]{1,0:T(8,128)(2,1)S(1)}, bf16[24,1024]{1,0:T(8,128)(2,1)S(1)}, u32[]{:S(2)}, u32[]{:S(2)}) collective-permute-start(bf16[24,1024]{1,0:T(8,128)(2,1)S(1)} %get-tuple-element.92), channel_id=1, source_target_pairs={{0,8},{1,9},{2,10},{3,11},{4,12},{5,13},{6,14},{7,15},{8,16},{9,17... | collective-permute-start | bytes 147464 | tf_op jit(solution)/shard_map/ppermute | solution.py:24
  106.4 5.7 %collective-permute-start.25 = (bf16[24,1024]{1,0:T(8,128)(2,1)S(1)}, bf16[24,1024]{1,0:T(8,128)(2,1)S(1)}, u32[]{:S(2)}, u32[]{:S(2)}) collective-permute-start(bf16[24,1024]{1,0:T(8,128)(2,1)S(1)} %fusion.5), channel_id=1, source_target_pairs={{0,64},{32,96},{64,0},{96,32},{1,65},{33,97},{65,1},{97,33},{2,66}... | collective-permute-start | bytes 147464 | tf_op jit(solution)/shard_map/ppermute | solution.py:24
  106.4 5.8 %collective-permute-start.24 = (bf16[24,1024]{1,0:T(8,128)(2,1)S(1)}, bf16[24,1024]{1,0:T(8,128)(2,1)S(1)}, u32[]{:S(2)}, u32[]{:S(2)}) collective-permute-start(bf16[24,1024]{1,0:T(8,128)(2,1)S(1)} %fusion.5), channel_id=1, source_target_pairs={{0,32},{32,64},{64,96},{96,0},{1,33},{33,65},{65,97},{97,1},{2,34}... | collective-permute-start | bytes 147464 | tf_op jit(solution)/shard_map/ppermute | solution.py:24
  (10 other events, 176.3 us)
